TPU v7x, 512 devices: a whole 4x8x8 slice. The times are simulated.
512 devices in a mesh: var: 64 (over x, y_hi, z), samp: 8 (over y_lo, core).
Axes of the slice: x: 4, y: 8 (y_hi: 2, y_lo: 4; y = y_hi * 4 + y_lo), z: 8, core: 2. Of those that a mesh axis runs over, the one named last changes fastest.
Arguments:
- data: float32 [2048, 32768], P('samp', 'var'), may hold values from -6 to 6
- tiles: float32 [64, 3, 512, 512], P('var'), as said below
- offsets: int32 [64, 3], P('var'), may hold values from 0 to 5, as said below
- step: float32 [1], replicated, may hold values from 0.3 to 0.7
Outputs:
- new_tiles: float32 [64, 3, 512, 512], P('var', None, 'samp')
Inputs may be any that keep to these rules, and one draw needn't show every extreme that they name: Slot 0 of every block row has offset 0. Every other slot holds 0 (empty) or an offset of 1 to 5; live slots come first in a row and their offsets differ. Some block row has all 3 slots live, one of them at offset 5. `tiles`: tiles of empty slots are zero. Slot 0 is symmetric with its diagonal between 1 and 2.
All inputs are finite; a program needn't handle non-finite values.
Results may differ from a plain program's by a relative error of at most 0.0003.
Values sent between devices are 32-bit elements; how exact they have to be, the bound alone decides.
A program may use at most 64 MiB of HBM per device.

v0:
```python
import jax
import jax.numpy as jnp
from jax import lax
from jax.sharding import PartitionSpec as P

BAND = 6


highest = lax.Precision.HIGHEST
penalty_weight = 0.05


def shifted(value, axis, steps):
    count = lax.axis_size(axis)
    pairs = [(source, (source + steps) % count) for source in range(count)]
    return lax.ppermute(value, axis, pairs)


def split_up(array, dim, size):
    lengths = array.shape
    parts = array.reshape(*lengths[:dim], size, lengths[dim] // size, *lengths[dim + 1 :])
    return jnp.moveaxis(parts, dim, 0)


def summed_on_arrival(array, axis, dim):
    parts = split_up(array, dim, lax.axis_size(axis))
    arrived = lax.all_to_all(parts, axis, split_axis=0, concat_axis=0, tiled=True)
    return arrived.sum(axis=0)


def shards(data, tiles, offsets, step):
    local_tiles = tiles[0]
    offset_row = offsets[0]
    slot_count = local_tiles.shape[0]
    block_size = local_tiles.shape[1]
    samp_count = lax.axis_size("samp")
    samples = data.shape[0] * samp_count
    step_size = step[0]
    slot_ids = jnp.arange(slot_count)
    onehot = (offset_row[:, None] == jnp.arange(BAND)[None, :]).astype(jnp.float32)
    active = ((slot_ids == 0) | (offset_row > 0)).astype(jnp.float32)
    mirror = (offset_row > 0).astype(jnp.float32)
    ahead_blocks = [data]
    for offset in range(1, BAND):
        ahead_blocks.append(shifted(ahead_blocks[-1], "var", -1))
    stacked = jnp.stack(ahead_blocks)
    partner = jnp.einsum(
        "jk,ksb->jsb", onehot, stacked, precision=highest, preferred_element_type=jnp.float32
    )
    forward = jnp.einsum(
        "sa,jab->jsb", data, local_tiles, precision=highest, preferred_element_type=jnp.float32
    )
    backward = jnp.einsum(
        "jsa,jba->jsb", partner, local_tiles, precision=highest, preferred_element_type=jnp.float32
    )
    image_local = forward[0] + jnp.einsum(
        "j,jsb->sb", mirror, backward, precision=highest, preferred_element_type=jnp.float32
    )
    send_parts = jnp.einsum(
        "jk,jsb->ksb", onehot, forward, precision=highest, preferred_element_type=jnp.float32
    )
    carried = jnp.zeros_like(image_local)
    for offset in range(BAND - 1, 0, -1):
        carried = shifted(carried + send_parts[offset], "var", 1)
    image_full = image_local + carried
    image_blocks = [image_full]
    for offset in range(1, BAND):
        image_blocks.append(shifted(image_blocks[-1], "var", -1))
    image_partner = jnp.einsum(
        "jk,ksb->jsb",
        onehot,
        jnp.stack(image_blocks),
        precision=highest,
        preferred_element_type=jnp.float32,
    )
    row_count = block_size // samp_count
    left_term = jnp.einsum(
        "sa,jsb->ajb", data, image_partner, precision=highest, preferred_element_type=jnp.float32
    )
    right_term = jnp.einsum(
        "sa,jsb->ajb", image_full, partner, precision=highest, preferred_element_type=jnp.float32
    )
    summed = summed_on_arrival(left_term + right_term, "samp", 0)
    gradient = summed / (2.0 * samples)
    row_start = lax.axis_index("samp") * row_count
    row_ids = row_start + jnp.arange(row_count)
    on_diag = row_ids[:, None] == jnp.arange(block_size)[None, :]
    diag_slot = on_diag[:, None, :] & (slot_ids == 0)[None, :, None]
    inverse = 1.0 / jnp.diagonal(local_tiles[0])
    gradient = gradient - jnp.where(diag_slot, inverse[None, None, :], 0.0)
    old_rows = jnp.transpose(
        lax.dynamic_slice_in_dim(local_tiles, row_start, row_count, 1), (1, 0, 2)
    )
    stepped = old_rows - step_size * gradient
    shrunk = jnp.sign(stepped) * jnp.maximum(jnp.abs(stepped) - step_size * penalty_weight, 0.0)
    result = jnp.where(diag_slot, stepped, shrunk) * active[None, :, None]
    return jnp.transpose(result, (1, 0, 2))[None]


def solution(mesh):
    return jax.shard_map(
        shards,
        mesh=mesh,
        in_specs=(P("samp", "var"), P("var", None, None, None), P("var", None), P()),
        out_specs=P("var", None, "samp", None),
        check_vma=False,
    )
```

profile of v0, /device:TPU:1, one launch (start us, length us, event | category | flops | bytes accessed | tf_op | source)
XLA Modules:
  0.0 430.3 jit_solution(8854872299656952026)
XLA Ops:
  0.0 18.9 %collective-permute-start = (f32[256,512]{1,0:T(8,128)}, f32[256,512]{1,0:T(8,128)}, u32[]{:S(2)}, u32[]{:S(2)}) collective-permute-start(f32[256,512]{1,0:T(8,128)} %param.4), channel_id=1, source_target_pairs={{0,504},{8,0},{16,8},{24,16},{32,24},{40,32},{48,40},{56,48},{64,5... | collective-permute-start | bytes 1572872 | tf_op jit(solution)/shard_map/ppermute | solution.py:16
  18.9 7.1 %fusion.8 = f32[3,256,512]{1,2,0:T(8,128)S(1)} fusion(f32[1,3,512,512]{3,2,1,0:T(8,128)} %param.5, f32[256,512]{1,0:T(8,128)} %param.4), kind=kOutput, calls=%fused_computation.10 | convolution fusion | flops 2415919104 | bytes 5242880 | tf_op jit(solution)/shard_map/sa,jab->jsb/dot_general | solution.py:50
  41.1 12.2 %collective-permute-start.1 = (f32[256,512]{1,0:T(8,128)}, f32[256,512]{1,0:T(8,128)}, u32[]{:S(2)}, u32[]{:S(2)}) collective-permute-start(f32[256,512]{1,0:T(8,128)} %collective-permute-done), channel_id=1, source_target_pairs={{0,504},{8,0},{16,8},{24,16},{32,24},{40,32},{48,40},{56,48},{64,5... | collective-permute-start | bytes 1572872 | tf_op jit(solution)/shard_map/ppermute | solution.py:16
  53.3 16.8 %collective-permute-done.5 = f32[256,512]{0,1:T(8,128)} collective-permute-done((f32[256,512]{0,1:T(8,128)S(1)}, f32[256,512]{0,1:T(8,128)}, u32[]{:S(2)}, u32[]{:S(2)}) %collective-permute-start.5) | collective-permute-done | bytes 524320 | tf_op jit(solution)/shard_map/ppermute | solution.py:16
  75.2 12.2 %collective-permute-start.2 = (f32[256,512]{1,0:T(8,128)}, f32[256,512]{1,0:T(8,128)}, u32[]{:S(2)}, u32[]{:S(2)}) collective-permute-start(f32[256,512]{1,0:T(8,128)} %collective-permute-done.1), channel_id=1, source_target_pairs={{0,504},{8,0},{16,8},{24,16},{32,24},{40,32},{48,40},{56,48},{64,5... | collective-permute-start | bytes 1572872 | tf_op jit(solution)/shard_map/ppermute | solution.py:16
  87.4 18.7 %collective-permute-done.6 = f32[256,512]{0,1:T(8,128)} collective-permute-done((f32[256,512]{0,1:T(8,128)S(1)}, f32[256,512]{0,1:T(8,128)}, u32[]{:S(2)}, u32[]{:S(2)}) %collective-permute-start.6) | collective-permute-done | bytes 524320 | tf_op jit(solution)/shard_map/ppermute | solution.py:16
  111.6 12.2 %collective-permute-start.3 = (f32[256,512]{1,0:T(8,128)}, f32[256,512]{1,0:T(8,128)}, u32[]{:S(2)}, u32[]{:S(2)}) collective-permute-start(f32[256,512]{1,0:T(8,128)} %collective-permute-done.2), channel_id=1, source_target_pairs={{0,504},{8,0},{16,8},{24,16},{32,24},{40,32},{48,40},{56,48},{64,5... | collective-permute-start | bytes 1572872 | tf_op jit(solution)/shard_map/ppermute | solution.py:16
  123.9 6.4 %collective-permute-done.7 = f32[256,512]{0,1:T(8,128)} collective-permute-done((f32[256,512]{0,1:T(8,128)S(1)}, f32[256,512]{0,1:T(8,128)}, u32[]{:S(2)}, u32[]{:S(2)}) %collective-permute-start.7) | collective-permute-done | bytes 524320 | tf_op jit(solution)/shard_map/ppermute | solution.py:16
  133.3 12.7 %collective-permute-done.3 = f32[256,512]{1,0:T(8,128)} collective-permute-done((f32[256,512]{1,0:T(8,128)}, f32[256,512]{1,0:T(8,128)}, u32[]{:S(2)}, u32[]{:S(2)}) %collective-permute-start.3) | collective-permute-done | bytes 524320 | tf_op jit(solution)/shard_map/ppermute | solution.py:16
  146.0 12.4 %collective-permute-start.4 = (f32[256,512]{1,0:T(8,128)}, f32[256,512]{1,0:T(8,128)}, u32[]{:S(2)}, u32[]{:S(2)}) collective-permute-start(f32[256,512]{1,0:T(8,128)} %collective-permute-done.3), channel_id=1, source_target_pairs={{0,504},{8,0},{16,8},{24,16},{32,24},{40,32},{48,40},{56,48},{64,5... | collective-permute-start | bytes 1572872 | tf_op jit(solution)/shard_map/ppermute | solution.py:16
  170.9 8.2 %stack.48 = f32[6,256,512]{2,0,1:T(8,128)} concatenate(f32[1,256,512]{2,0,1:T(1,128)S(1)} %stack.42, f32[1,256,512]{2,0,1:T(1,128)S(1)} %copy.32, f32[1,256,512]{2,0,1:T(1,128)S(1)} %copy.33, f32[1,256,512]{2,0,1:T(1,128)S(1)} %copy.34, f32[1,256,512]{2,0,1:T(1,128)S(1)} %copy.35, f32[1,256,512]{2,0,1:T(1,128)S(1)} %stack.47), dimensions={0} | concatenate | bytes 6291456 | tf_op jit(solution)/shard_map/stack | solution.py:46
  195.4 11.5 %collective-permute-start.10 = (f32[256,512]{0,1:T(8,128)S(1)}, f32[256,512]{0,1:T(8,128)S(1)}, u32[]{:S(2)}, u32[]{:S(2)}) collective-permute-start(f32[256,512]{0,1:T(8,128)S(1)} %get-tuple-element.6), channel_id=1, source_target_pairs={{0,504},{8,0},{16,8},{24,16},{32,24},{40,32},{48,40},{56,48},{64,5... | collective-permute-start | bytes 1572872 | tf_op jit(solution)/shard_map/ppermute | solution.py:16
  206.9 21.1 %collective-permute-done.10 = f32[256,512]{0,1:T(8,128)S(1)} collective-permute-done((f32[256,512]{0,1:T(8,128)S(1)}, f32[256,512]{0,1:T(8,128)S(1)}, u32[]{:S(2)}, u32[]{:S(2)}) %collective-permute-start.10) | collective-permute-done | bytes 524320 | tf_op jit(solution)/shard_map/ppermute | solution.py:16
  227.9 12.2 %collective-permute-start.11 = (f32[256,512]{0,1:T(8,128)S(1)}, f32[256,512]{0,1:T(8,128)S(1)}, u32[]{:S(2)}, u32[]{:S(2)}) collective-permute-start(f32[256,512]{0,1:T(8,128)S(1)} %collective-permute-done.10), channel_id=1, source_target_pairs={{0,504},{8,0},{16,8},{24,16},{32,24},{40,32},{48,40},{56,48},{64,5... | collective-permute-start | bytes 1572872 | tf_op jit(solution)/shard_map/ppermute | solution.py:16
  240.2 17.9 %collective-permute-done.11 = f32[256,512]{0,1:T(8,128)S(1)} collective-permute-done((f32[256,512]{0,1:T(8,128)S(1)}, f32[256,512]{0,1:T(8,128)S(1)}, u32[]{:S(2)}, u32[]{:S(2)}) %collective-permute-start.11) | collective-permute-done | bytes 524320 | tf_op jit(solution)/shard_map/ppermute | solution.py:16
  258.1 12.4 %collective-permute-start.12 = (f32[256,512]{0,1:T(8,128)S(1)}, f32[256,512]{0,1:T(8,128)S(1)}, u32[]{:S(2)}, u32[]{:S(2)}) collective-permute-start(f32[256,512]{0,1:T(8,128)S(1)} %collective-permute-done.11), channel_id=1, source_target_pairs={{0,504},{8,0},{16,8},{24,16},{32,24},{40,32},{48,40},{56,48},{64,5... | collective-permute-start | bytes 1572872 | tf_op jit(solution)/shard_map/ppermute | solution.py:16
  270.5 10.6 %collective-permute-done.12 = f32[256,512]{0,1:T(8,128)S(1)} collective-permute-done((f32[256,512]{0,1:T(8,128)S(1)}, f32[256,512]{0,1:T(8,128)S(1)}, u32[]{:S(2)}, u32[]{:S(2)}) %collective-permute-start.12) | collective-permute-done | bytes 524320 | tf_op jit(solution)/shard_map/ppermute | solution.py:16
  281.1 12.4 %collective-permute-start.13 = (f32[256,512]{0,1:T(8,128)S(1)}, f32[256,512]{0,1:T(8,128)S(1)}, u32[]{:S(2)}, u32[]{:S(2)}) collective-permute-start(f32[256,512]{0,1:T(8,128)S(1)} %collective-permute-done.12), channel_id=1, source_target_pairs={{0,504},{8,0},{16,8},{24,16},{32,24},{40,32},{48,40},{56,48},{64,5... | collective-permute-start | bytes 1572872 | tf_op jit(solution)/shard_map/ppermute | solution.py:16
  294.4 13.6 %collective-permute-done.13 = f32[256,512]{0,1:T(8,128)S(1)} collective-permute-done((f32[256,512]{0,1:T(8,128)S(1)}, f32[256,512]{0,1:T(8,128)S(1)}, u32[]{:S(2)}, u32[]{:S(2)}) %collective-permute-start.13) | collective-permute-done | bytes 524320 | tf_op jit(solution)/shard_map/ppermute | solution.py:16
  307.9 12.4 %collective-permute-start.14 = (f32[256,512]{0,1:T(8,128)S(1)}, f32[256,512]{0,1:T(8,128)S(1)}, u32[]{:S(2)}, u32[]{:S(2)}) collective-permute-start(f32[256,512]{0,1:T(8,128)S(1)} %collective-permute-done.13), channel_id=1, source_target_pairs={{0,504},{8,0},{16,8},{24,16},{32,24},{40,32},{48,40},{56,48},{64,5... | collective-permute-start | bytes 1572872 | tf_op jit(solution)/shard_map/ppermute | solution.py:16
  322.9 8.0 %collective-permute-done.14 = f32[256,512]{0,1:T(8,128)S(1)} collective-permute-done((f32[256,512]{0,1:T(8,128)S(1)}, f32[256,512]{0,1:T(8,128)S(1)}, u32[]{:S(2)}, u32[]{:S(2)}) %collective-permute-start.14) | collective-permute-done | bytes 524320 | tf_op jit(solution)/shard_map/ppermute | solution.py:16
  349.8 5.7 %all-to-all-start = ((f32[8,64,3,512]{3,1,2,0:T(8,128)}), f32[8,64,3,512]{3,1,2,0:T(8,128)}, u32[]{:S(2)}, u32[]{:S(2)}) async-start(f32[8,64,3,512]{3,1,2,0:T(8,128)} %copy.47), calls=%async_computation | async-start | bytes 6291456 | tf_op jit(solution)/shard_map/all_to_all | solution.py:27
  357.2 8.9 %gather_fusion = f32[512]{0:T(512)S(1)} fusion(f32[512,512]{1,0:T(8,128)} %slice_bitcast_fusion, s32[512]{0:T(512)S(1)} %bitcast.89), kind=kCustom, calls=%fused_computation | custom fusion | bytes 8192 | tf_op jit(solution)/shard_map/jit(diagonal)/cond/branch_0_fun/gather | solution.py:89
  366.8 59.3 %all-to-all-done = f32[8,64,3,512]{3,1,2,0:T(8,128)} async-done(((f32[8,64,3,512]{3,1,2,0:T(8,128)}), f32[8,64,3,512]{3,1,2,0:T(8,128)}, u32[]{:S(2)}, u32[]{:S(2)}) %all-to-all-start) | async-done | bytes 3145760 | tf_op jit(solution)/shard_map/all_to_all | solution.py:27
  (70 shorter events, 85.3 us)
Async XLA Ops:
  0.0 41.1 %collective-permute-start = (f32[256,512]{1,0:T(8,128)}, f32[256,512]{1,0:T(8,128)}, u32[]{:S(2)}, u32[]{:S(2)}) collective-permute-start(f32[256,512]{1,0:T(8,128)} %param.4), channel_id=1, source_target_pairs={{0,504},{8,0},{16,8},{24,16},{32,24},{40,32},{48,40},{56,48},{64,5... | collective-permute-start | bytes 1572872 | tf_op jit(solution)/shard_map/ppermute | solution.py:16
  26.0 6.1 %copy-start.3 = (f32[3,256,512]{1,2,0:T(8,128)}, f32[3,256,512]{1,2,0:T(8,128)S(1)}, u32[]{:S(2)}) copy-start(f32[3,256,512]{1,2,0:T(8,128)S(1)} %fusion.8) | copy-start | bytes 4718596
  26.0 1.9 copy-start.8
  36.2 33.8 %collective-permute-start.5 = (f32[256,512]{0,1:T(8,128)S(1)}, f32[256,512]{0,1:T(8,128)}, u32[]{:S(2)}, u32[]{:S(2)}) collective-permute-start(f32[256,512]{0,1:T(8,128)S(1)} %bitcast.91), channel_id=1, source_target_pairs={{0,8},{8,16},{16,24},{24,32},{32,40},{40,48},{48,56},{56,64},{64,7... | collective-permute-start | bytes 1572872 | tf_op jit(solution)/shard_map/ppermute | solution.py:16
  39.4 119.0 %copy-start.4 = (f32[256,512]{1,0:T(8,128)S(1)}, f32[256,512]{1,0:T(8,128)}, u32[]{:S(2)}) copy-start(f32[256,512]{1,0:T(8,128)} %param.4) | copy-start | bytes 1572868
  41.1 34.1 %collective-permute-start.1 = (f32[256,512]{1,0:T(8,128)}, f32[256,512]{1,0:T(8,128)}, u32[]{:S(2)}, u32[]{:S(2)}) collective-permute-start(f32[256,512]{1,0:T(8,128)} %collective-permute-done), channel_id=1, source_target_pairs={{0,504},{8,0},{16,8},{24,16},{32,24},{40,32},{48,40},{56,48},{64,5... | collective-permute-start | bytes 1572872 | tf_op jit(solution)/shard_map/ppermute | solution.py:16
  71.2 35.0 %collective-permute-start.6 = (f32[256,512]{0,1:T(8,128)S(1)}, f32[256,512]{0,1:T(8,128)}, u32[]{:S(2)}, u32[]{:S(2)}) collective-permute-start(f32[256,512]{0,1:T(8,128)S(1)} %bitcast_add_fusion.4), channel_id=1, source_target_pairs={{0,8},{8,16},{16,24},{24,32},{32,40},{40,48},{48,56},{56,64},{64,7... | collective-permute-start | bytes 1572872 | tf_op jit(solution)/shard_map/ppermute | solution.py:16
  75.2 36.4 %collective-permute-start.2 = (f32[256,512]{1,0:T(8,128)}, f32[256,512]{1,0:T(8,128)}, u32[]{:S(2)}, u32[]{:S(2)}) collective-permute-start(f32[256,512]{1,0:T(8,128)} %collective-permute-done.1), channel_id=1, source_target_pairs={{0,504},{8,0},{16,8},{24,16},{32,24},{40,32},{48,40},{56,48},{64,5... | collective-permute-start | bytes 1572872 | tf_op jit(solution)/shard_map/ppermute | solution.py:16
  107.3 23.0 %collective-permute-start.7 = (f32[256,512]{0,1:T(8,128)S(1)}, f32[256,512]{0,1:T(8,128)}, u32[]{:S(2)}, u32[]{:S(2)}) collective-permute-start(f32[256,512]{0,1:T(8,128)S(1)} %bitcast_add_fusion.3), channel_id=1, source_target_pairs={{0,8},{8,16},{16,24},{24,32},{32,40},{40,48},{48,56},{56,64},{64,7... | collective-permute-start | bytes 1572872 | tf_op jit(solution)/shard_map/ppermute | solution.py:16
  111.6 34.4 %collective-permute-start.3 = (f32[256,512]{1,0:T(8,128)}, f32[256,512]{1,0:T(8,128)}, u32[]{:S(2)}, u32[]{:S(2)}) collective-permute-start(f32[256,512]{1,0:T(8,128)} %collective-permute-done.2), channel_id=1, source_target_pairs={{0,504},{8,0},{16,8},{24,16},{32,24},{40,32},{48,40},{56,48},{64,5... | collective-permute-start | bytes 1572872 | tf_op jit(solution)/shard_map/ppermute | solution.py:16
  131.4 32.6 %collective-permute-start.8 = (f32[256,512]{0,1:T(8,128)S(1)}, f32[256,512]{0,1:T(8,128)}, u32[]{:S(2)}, u32[]{:S(2)}) collective-permute-start(f32[256,512]{0,1:T(8,128)S(1)} %bitcast_add_fusion.2), channel_id=1, source_target_pairs={{0,8},{8,16},{16,24},{24,32},{32,40},{40,48},{48,56},{56,64},{64,7... | collective-permute-start | bytes 1572872 | tf_op jit(solution)/shard_map/ppermute | solution.py:16
  146.0 23.5 %collective-permute-start.4 = (f32[256,512]{1,0:T(8,128)}, f32[256,512]{1,0:T(8,128)}, u32[]{:S(2)}, u32[]{:S(2)}) collective-permute-start(f32[256,512]{1,0:T(8,128)} %collective-permute-done.3), channel_id=1, source_target_pairs={{0,504},{8,0},{16,8},{24,16},{32,24},{40,32},{48,40},{56,48},{64,5... | collective-permute-start | bytes 1572872 | tf_op jit(solution)/shard_map/ppermute | solution.py:16
  166.0 26.3 %collective-permute-start.9 = (f32[256,512]{0,1:T(8,128)}, f32[256,512]{0,1:T(8,128)}, u32[]{:S(2)}, u32[]{:S(2)}) collective-permute-start(f32[256,512]{0,1:T(8,128)} %bitcast_add_fusion.1), channel_id=1, source_target_pairs={{0,8},{8,16},{16,24},{24,32},{32,40},{40,48},{48,56},{56,64},{64,7... | collective-permute-start | bytes 1572872 | tf_op jit(solution)/shard_map/ppermute | solution.py:16
  179.1 4.4 %copy-start = (f32[1,3,512,512]{3,2,1,0:T(8,128)S(1)}, f32[1,3,512,512]{3,2,1,0:T(8,128)}, u32[]{:S(2)}) copy-start(f32[1,3,512,512]{3,2,1,0:T(8,128)} %param.5) | copy-start | bytes 9437188
  183.5 3.3 copy-start.1
  195.4 32.6 %collective-permute-start.10 = (f32[256,512]{0,1:T(8,128)S(1)}, f32[256,512]{0,1:T(8,128)S(1)}, u32[]{:S(2)}, u32[]{:S(2)}) collective-permute-start(f32[256,512]{0,1:T(8,128)S(1)} %get-tuple-element.6), channel_id=1, source_target_pairs={{0,504},{8,0},{16,8},{24,16},{32,24},{40,32},{48,40},{56,48},{64,5... | collective-permute-start | bytes 1572872 | tf_op jit(solution)/shard_map/ppermute | solution.py:16
  227.9 30.1 %collective-permute-start.11 = (f32[256,512]{0,1:T(8,128)S(1)}, f32[256,512]{0,1:T(8,128)S(1)}, u32[]{:S(2)}, u32[]{:S(2)}) collective-permute-start(f32[256,512]{0,1:T(8,128)S(1)} %collective-permute-done.10), channel_id=1, source_target_pairs={{0,504},{8,0},{16,8},{24,16},{32,24},{40,32},{48,40},{56,48},{64,5... | collective-permute-start | bytes 1572872 | tf_op jit(solution)/shard_map/ppermute | solution.py:16
  258.1 23.0 %collective-permute-start.12 = (f32[256,512]{0,1:T(8,128)S(1)}, f32[256,512]{0,1:T(8,128)S(1)}, u32[]{:S(2)}, u32[]{:S(2)}) collective-permute-start(f32[256,512]{0,1:T(8,128)S(1)} %collective-permute-done.11), channel_id=1, source_target_pairs={{0,504},{8,0},{16,8},{24,16},{32,24},{40,32},{48,40},{56,48},{64,5... | collective-permute-start | bytes 1572872 | tf_op jit(solution)/shard_map/ppermute | solution.py:16
  281.1 26.8 %collective-permute-start.13 = (f32[256,512]{0,1:T(8,128)S(1)}, f32[256,512]{0,1:T(8,128)S(1)}, u32[]{:S(2)}, u32[]{:S(2)}) collective-permute-start(f32[256,512]{0,1:T(8,128)S(1)} %collective-permute-done.12), channel_id=1, source_target_pairs={{0,504},{8,0},{16,8},{24,16},{32,24},{40,32},{48,40},{56,48},{64,5... | collective-permute-start | bytes 1572872 | tf_op jit(solution)/shard_map/ppermute | solution.py:16
  307.9 23.0 %collective-permute-start.14 = (f32[256,512]{0,1:T(8,128)S(1)}, f32[256,512]{0,1:T(8,128)S(1)}, u32[]{:S(2)}, u32[]{:S(2)}) collective-permute-start(f32[256,512]{0,1:T(8,128)S(1)} %collective-permute-done.13), channel_id=1, source_target_pairs={{0,504},{8,0},{16,8},{24,16},{32,24},{40,32},{48,40},{56,48},{64,5... | collective-permute-start | bytes 1572872 | tf_op jit(solution)/shard_map/ppermute | solution.py:16
  337.0 4.3 %copy-start.5 = (f32[256,512]{1,0:T(8,128)S(1)}, f32[256,512]{1,0:T(8,128)}, u32[]{:S(2)}) copy-start(f32[256,512]{1,0:T(8,128)} %param.4) | copy-start | bytes 1572868
  341.4 3.3 copy-start.2
  341.4 3.3 copy-start.7
  349.8 76.4 %all-to-all-start = ((f32[8,64,3,512]{3,1,2,0:T(8,128)}), f32[8,64,3,512]{3,1,2,0:T(8,128)}, u32[]{:S(2)}, u32[]{:S(2)}) async-start(f32[8,64,3,512]{3,1,2,0:T(8,128)} %copy.47), calls=%async_computation | async-start | bytes 6291456 | tf_op jit(solution)/shard_map/all_to_all | solution.py:27
  (1 other events, 0.8 us)
where the time goes:
time: 432 us; the launch traced here: 430 us
  waiting for transfers between devices  190 us (44%)
  starting transfers between devices  144 us (33%)
  local copies, waits for them, and re-layouts  49 us (11%)
  matrix products  33.3 us (8%)
  other arithmetic  12.3 us (3%)
    ppermute x15, starting transfers between devices, shifted(): return lax.ppermute(value, axis, pairs)  139 us
    ppermute x15, waiting for transfers between devices, shifted(): return lax.ppermute(value, axis, pairs)  131 us
    all_to_all x1, waiting for transfers between devices, summed_on_arrival(): lax.all_to_all(parts, axis, split_axis=0, concat_axis=0, tiled=True)  59.3 us
    another operation x7, local copies, waits for them, and re-layouts, shards(): stacked = jnp.stack(ahead_blocks)  16.2 us
    gather x1, local copies, waits for them, and re-layouts, shards(): inverse = 1.0 / jnp.diagonal(local_tiles[0])  8.89 us
  transfers between devices with their start and end apart: 16, of which 13 were waited for; matrix products, arithmetic and copies ran while one was open for 16% of the time, Pallas kernels for 0%

commit v1 on v0

v1 whole, which is shorter than its diff:
```python
import functools
import jax
import jax.numpy as jnp
from jax import lax
from jax.experimental import pallas as pl
from jax.experimental.pallas import tpu as pltpu
from jax.sharding import PartitionSpec as P

BAND = 6
MESH = pl.DeviceIdType.MESH
RING = 8
WRAP = 2
CHUNKS = 4


def var_device(index):
    return {"var": index}


def band_kernel(wrap, chunks, reduce_too, *refs):
    if reduce_too:
        (data_ref, first_ref, second_ref, mask_ref, ahead_ref, carried_ref,
         sent_ref, near_ref, far_ref, cross_ref,
         d_send, d_recv, d_direct, d_back,
         c_send, c_near, c_far, c_cross) = refs
    else:
        data_ref, ahead_ref, d_send, d_recv, d_direct, d_back = refs
    count = lax.axis_size("var")
    me = lax.axis_index("var")
    z = lax.rem(me, RING)
    before, after = lax.rem(me + count - 1, count), lax.rem(me + 1, count)
    left5, right5 = lax.rem(me + count - 5, count), lax.rem(me + 5, count)
    rows = data_ref.shape[0] // chunks
    edge = 7 + wrap

    barrier = pltpu.get_barrier_semaphore()
    for other in (before, after, left5, right5):
        pl.semaphore_signal(barrier, inc=1, device_id=var_device(other), device_id_type=MESH)
    pl.semaphore_wait(barrier, 4)

    def part(k):
        return pl.ds(pl.multiple_of(k * rows, rows), rows)

    def natural(t, k):
        source = data_ref.at[part(k)] if t == 0 else ahead_ref.at[t - 1, part(k)]
        return pltpu.make_async_remote_copy(
            src_ref=source, dst_ref=ahead_ref.at[t, part(k)],
            send_sem=d_send.at[t, k], recv_sem=d_recv.at[t, k],
            device_id=var_device(before), device_id_type=MESH)

    def direct(k):
        return pltpu.make_async_remote_copy(
            src_ref=data_ref.at[part(k)], dst_ref=ahead_ref.at[4, part(k)],
            send_sem=d_direct.at[k], recv_sem=d_recv.at[4, k],
            device_id=var_device(left5), device_id_type=MESH)

    def back(t, k):
        return pltpu.make_async_remote_copy(
            src_ref=ahead_ref.at[t - 1, part(k)], dst_ref=ahead_ref.at[t - 2, part(k)],
            send_sem=d_back.at[t - 2, k], recv_sem=d_recv.at[t - 2, k],
            device_id=var_device(after), device_id_type=MESH)

    def goes_on(t):
        return ((z >= 1) & (z + t <= edge)) | ((z == 0) & (t + 1 <= wrap))

    sends_direct = (z >= wrap) & (z <= 4)

    def arrived(t, k):
        natural(t - 1, k).wait_recv()

    def own(o, k):
        return mask_ref[2 * o : 2 * o + 1] * first_ref[part(k)] + mask_ref[2 * o + 1 : 2 * o + 2] * second_ref[part(k)]

    def pass_on(o, k):
        return pltpu.make_async_remote_copy(
            src_ref=sent_ref.at[o - 1, part(k)], dst_ref=near_ref.at[o - 1, part(k)],
            send_sem=c_send.at[o - 1, k], recv_sem=c_near.at[o - 1, k],
            device_id=var_device(after), device_id_type=MESH)

    def pass_back(o, k):
        return pltpu.make_async_remote_copy(
            src_ref=sent_ref.at[o - 1, part(k)], dst_ref=far_ref.at[o, part(k)],
            send_sem=c_send.at[o - 1, k], recv_sem=c_far.at[o, k],
            device_id=var_device(before), device_id_type=MESH)

    def pass_cross(k):
        return pltpu.make_async_remote_copy(
            src_ref=sent_ref.at[4, part(k)], dst_ref=cross_ref.at[part(k)],
            send_sem=c_send.at[4, k], recv_sem=c_cross.at[k],
            device_id=var_device(right5), device_id_type=MESH)

    def passes(o):
        return ((z <= 6) & (z + o <= edge)) | ((z == 7) & (o <= wrap))

    def has_near(o):
        return (o < 5) & (((z >= 1) & (z + o <= edge)) | ((z == 0) & (o + 1 <= wrap)))

    def loop(body):
        def step(k, carry):
            body(k)
            return carry
        lax.fori_loop(0, chunks, step, 0)

    def first(k):
        natural(0, k).start()

        @pl.when(sends_direct)
        def _():
            direct(k).start()

        if reduce_too:
            sent_ref[4, part(k)] = own(5, k)

            @pl.when(passes(5))
            def _():
                pass_on(5, k).start()

            @pl.when(z == 7)
            def _():
                for o in range(wrap + 1, 5):
                    sent_ref[o - 1, part(k)] = own(o, k)
                    pass_back(o, k).start()
                if wrap < 5:
                    pass_cross(k).start()

    loop(first)

    for tau in range(1, 6):
        cross_t = 7 - tau

        def step(k, tau=tau, cross_t=cross_t):
            @pl.when(z + tau <= edge)
            def _():
                arrived(tau, k)

            if tau <= 4:
                @pl.when(goes_on(tau))
                def _():
                    natural(tau, k).start()

            if reduce_too and tau <= 4:
                o = 5 - tau

                @pl.when(passes(o))
                def _():
                    @pl.when(has_near(o))
                    def _():
                        pass_on(o + 1, k).wait_recv()
                        sent_ref[o - 1, part(k)] = near_ref[o, part(k)] + own(o, k)

                    @pl.when(jnp.logical_not(has_near(o)))
                    def _():
                        sent_ref[o - 1, part(k)] = own(o, k)

                    pass_on(o, k).start()

            if reduce_too and tau <= 4:
                place = 7 - tau
                for o in range(wrap + 1 + tau, 6):
                    @pl.when(z == place)
                    def _(o=o):
                        pass_back(o - 1, k).wait_recv()
                        sent_ref[o - 1, part(k)] = far_ref[o - 1, part(k)] + own(o, k)
                        if o < 5:
                            pass_back(o, k).start()
                        else:
                            pass_cross(k).start()

            if 2 <= tau and cross_t > wrap:
                @pl.when(z + cross_t > edge)
                def _():
                    arrived(cross_t, k)
                    if cross_t >= 2:
                        @pl.when(z <= 6)
                        def _():
                            back(cross_t, k).start()

        loop(step)

    if reduce_too:
        def final(k):
            pass_on(1, k).wait_recv()
            carried_ref[part(k)] = near_ref[0, part(k)]

            @pl.when(sends_direct)
            def _():
                pass_cross(k).wait_recv()
                carried_ref[part(k)] += cross_ref[part(k)]

        loop(final)

    def drain(k):
        natural(0, k).wait_send()

        @pl.when(sends_direct)
        def _():
            direct(k).wait_send()

        for t in range(1, 5):
            @pl.when(goes_on(t))
            def _(t=t):
                natural(t, k).wait_send()

        for t in range(wrap + 1, 6):
            if t >= 2:
                @pl.when((z + t > edge) & (z <= 6))
                def _(t=t):
                    back(t, k).wait_send()

        if reduce_too:
            for o in range(1, 6):
                @pl.when(passes(o) | (z + o > edge))
                def _(o=o):
                    pass_on(o, k).wait_send()

    loop(drain)


def band_call(data, sums, masks, wrap, chunks, reduce_too, collective_id):
    rows, size = data.shape
    dtype = data.dtype
    sem = pltpu.SemaphoreType.DMA
    block = jax.ShapeDtypeStruct((rows, size), dtype)
    ahead = jax.ShapeDtypeStruct((5, rows, size), dtype)
    vm = pl.BlockSpec(memory_space=pltpu.VMEM)
    base = [sem((5, chunks)), sem((5, chunks)), sem((chunks,)), sem((4, chunks))]
    if reduce_too:
        scratch = [pltpu.VMEM((5, rows, size), dtype)] * 3 + [pltpu.VMEM((rows, size), dtype)] + base + [
            sem((5, chunks)), sem((5, chunks)), sem((5, chunks)), sem((chunks,))]
        args, outs, specs = (data, *sums, masks), (ahead, block), (vm, vm)
    else:
        scratch, args, outs, specs = base, (data,), ahead, vm
    return pl.pallas_call(
        functools.partial(band_kernel, wrap, chunks, reduce_too),
        out_shape=outs, in_specs=[vm] * len(args), out_specs=specs, scratch_shapes=scratch,
        compiler_params=pltpu.CompilerParams(collective_id=collective_id, has_side_effects=True),
    )(*args)


def sum_kernel(grad_ref, out_ref, pair_ref, sent_ref, up_ref, down_ref,
               p_send, p_recv, u_send, u_recv, d_send, d_recv):
    me = lax.axis_index("samp")
    core = lax.rem(me, 2)
    y = me // 2
    places = lax.axis_size("samp") // 2
    rows = out_ref.shape[1]
    twin = me + 1 - 2 * core

    barrier = pltpu.get_barrier_semaphore()

    def greet(other):
        pl.semaphore_signal(barrier, inc=1, device_id={"samp": other}, device_id_type=MESH)

    greet(twin)

    @pl.when(y < places - 1)
    def _():
        greet(me + 2)

    @pl.when(y > 0)
    def _():
        greet(me - 2)

    peers = 1 + lax.min(y, 1) + lax.min(places - 1 - y, 1)
    pl.semaphore_wait(barrier, peers)

    def band(place, which):
        return pl.ds(pl.multiple_of((2 * place + which) * rows, rows), rows)

    def to_twin(place):
        return pltpu.make_async_remote_copy(
            src_ref=grad_ref.at[:, band(place, 1 - core)], dst_ref=pair_ref.at[place],
            send_sem=p_send.at[place], recv_sem=p_recv.at[place],
            device_id={"samp": twin}, device_id_type=MESH)

    def up(place):
        return pltpu.make_async_remote_copy(
            src_ref=sent_ref.at[place], dst_ref=up_ref.at[place],
            send_sem=u_send.at[place], recv_sem=u_recv.at[place],
            device_id={"samp": me + 2}, device_id_type=MESH)

    def down(place):
        return pltpu.make_async_remote_copy(
            src_ref=sent_ref.at[place], dst_ref=down_ref.at[place],
            send_sem=d_send.at[place], recv_sem=d_recv.at[place],
            device_id={"samp": me - 2}, device_id_type=MESH)

    order = []
    for j in range(places - 1):
        order += [places - 1 - j, j]
    starts = list(dict.fromkeys(order))
    for place in starts:
        to_twin(place).start()

    for j in range(places - 1):
        for rising in (True, False):
            place = places - 1 - j if rising else j

            @pl.when(y < place if rising else y > place)
            def _(place=place, rising=rising):
                to_twin(place).wait_recv()
                sent_ref[place] = grad_ref[:, band(place, core)] + pair_ref[place]

                @pl.when(y > 0 if rising else y < places - 1)
                def _():
                    if rising:
                        up(place).wait_recv()
                        sent_ref[place] += up_ref[place]
                    else:
                        down(place).wait_recv()
                        sent_ref[place] += down_ref[place]

                (up if rising else down)(place).start()

    for place in range(places):
        @pl.when(y == place)
        def _(place=place):
            to_twin(place).wait_recv()
            out_ref[...] = grad_ref[:, band(place, core)] + pair_ref[place]
            if place > 0:
                up(place).wait_recv()
                out_ref[...] += up_ref[place]
            if place < places - 1:
                down(place).wait_recv()
                out_ref[...] += down_ref[place]

    for place in range(places):
        to_twin(place).wait_send()

        @pl.when(y < place)
        def _(place=place):
            up(place).wait_send()

        @pl.when(y > place)
        def _(place=place):
            down(place).wait_send()


def sum_call(grad, collective_id):
    slots, size, width = grad.shape
    count = lax.axis_size("samp")
    rows = size // count
    sem = pltpu.SemaphoreType.DMA
    vm = pl.BlockSpec(memory_space=pltpu.VMEM)
    places = count // 2
    buffer = pltpu.VMEM((places, slots, rows, width), grad.dtype)
    return pl.pallas_call(
        sum_kernel,
        out_shape=jax.ShapeDtypeStruct((slots, rows, width), grad.dtype),
        in_specs=[vm], out_specs=vm,
        scratch_shapes=[buffer] * 4 + [sem((places,))] * 6,
        compiler_params=pltpu.CompilerParams(collective_id=collective_id, has_side_effects=True),
    )(grad)


high = lax.Precision.HIGH
penalty_weight = 0.05


def product(left, right, left_dim, right_dim):
    return lax.dot_general(left, right, (((left_dim,), (right_dim,)), ((), ())),
                           precision=high, preferred_element_type=jnp.float32)


def picked(offset, own, ahead):
    block = own
    for o in range(1, BAND):
        block = jnp.where(offset == o, ahead[o - 1], block)
    return block


def shards(data, tiles, offsets, step):
    tiles = tiles[0]
    offset = offsets[0]
    slots, size = tiles.shape[0], tiles.shape[1]
    samp_count = lax.axis_size("samp")
    samples = data.shape[0] * samp_count
    step_size = step[0]
    forward = [product(data, tiles[j], 1, 0) for j in range(slots)]
    places = jnp.arange(16) // 2
    slot_of_row = 1 + jnp.arange(16) % 2
    live = ((offset[slot_of_row] == places) & (places > 0)).astype(jnp.float32)
    masks = jnp.broadcast_to(live[:, None], (16, size))
    ahead, carried = band_call(data, forward[1:], masks, WRAP, CHUNKS, True, 1)
    partners = [data] + [picked(offset[j], data, ahead) for j in range(1, slots)]
    image = forward[0] + carried
    for j in range(1, slots):
        image = image + product(partners[j], tiles[j], 1, 1)
    image_ahead = band_call(image, None, None, WRAP, CHUNKS, False, 2)
    image_partners = [image] + [picked(offset[j], image, image_ahead) for j in range(1, slots)]
    grad = jnp.stack([product(data, image_partners[j], 0, 0) + product(image, partners[j], 0, 0) for j in range(slots)])
    summed = sum_call(grad, 3)
    rows = size // samp_count
    row_start = lax.axis_index("samp") * rows
    old = lax.dynamic_slice_in_dim(tiles, row_start, rows, 1)
    slot_ids = jnp.arange(slots)
    on_diag = (row_start + jnp.arange(rows))[:, None] == jnp.arange(size)[None, :]
    diag = on_diag[None] & (slot_ids == 0)[:, None, None]
    gradient = summed / (2.0 * samples) - jnp.where(diag, 1.0 / jnp.where(diag, old, 1.0), 0.0)
    stepped = old - step_size * gradient
    shrunk = jnp.sign(stepped) * jnp.maximum(jnp.abs(stepped) - step_size * penalty_weight, 0.0)
    active = (slot_ids == 0) | (offset > 0)
    return jnp.where(active[:, None, None], jnp.where(diag, stepped, shrunk), 0.0)[None]


def solution(mesh):
    return jax.shard_map(
        shards,
        mesh=mesh,
        in_specs=(P("samp", "var"), P("var", None, None, None), P("var", None), P()),
        out_specs=P("var", None, "samp", None),
        check_vma=False,
    )
```

time: 432 us -> 282 us (0.65)
  the two profiles are of different devices: /device:TPU:1 before, /device:TPU:305 now
where the time goes in v1:
time: 282 us
  Pallas kernels  246 us (87%)
  matrix products  18.6 us (7%)
  other arithmetic  7.09 us (3%)
  between operations  7.02 us (2%)
  local copies, waits for them, and re-layouts  3 us (1%)
    pallas_call x2, Pallas kernels, band_call(): pl.pallas_call(functools.partial(band_kernel, wrap, chunks, reduce_too),...  198 us
    pallas_call x1, Pallas kernels, sum_call(): pl.pallas_call(sum_kernel, out_shape=jax.ShapeDtypeStruct((slots, rows, w...  47.8 us
    dot_general x10, matrix products, product(): lax.dot_general(left, right, (((left_dim,), (right_dim,)), ((), ())), pre...  18.6 us

profile of v1, /device:TPU:305, one launch (start us, length us, event | category | flops | bytes accessed | tf_op | source)
XLA Modules:
  0.0 281.5 jit_solution(14592363010109998068)
XLA Ops:
  0.0 2.9 %fusion.7.refs_1_ = f32[256,512]{1,0:T(8,128)} fusion(f32[256,512]{1,0:T(8,128)} %refs_0_.1, f32[1,3,512,512]{3,2,1,0:T(8,128)} %param.5), kind=kOutput, calls=%fused_computation.16 | convolution fusion | flops 402653184 | bytes 2097152 | tf_op jit(solution)/shard_map/dot_general | solution.py:361
  2.9 2.8 fusion.4.refs_2_
  5.7 0.7 fusion.68
  6.3 1.9 and_convert_fusion
  8.2 0.7 broadcast_in_dim.20.refs_3_
  8.9 98.3 %shard_map.46 = (f32[5,256,512]{2,1,0:T(8,128)}, f32[256,512]{1,0:T(8,128)}) custom-call(f32[256,512]{1,0:T(8,128)} %refs_0_.1, f32[256,512]{1,0:T(8,128)} %fusion.7.refs_1_, f32[256,512]{1,0:T(8,128)} %fusion.4.refs_2_, f32[16,512]{1,0:T(8,128)} %broadcast_in_dim.20.refs_3_), custom_call_target="tpu_custom_call" | custom-call | tf_op jit(solution)/shard_map/pallas_call | solution.py:233
  107.3 2.1 convolution_add_fusion.4
  112.8 0.4 fusion.36
  113.2 0.7 convolution_add_fusion.3
  116.7 0.4 fusion.40
  117.0 1.5 convolution_add_fusion.2.refs_0_
  118.5 99.6 %shard_map.47 = f32[5,256,512]{2,1,0:T(8,128)} custom-call(f32[256,512]{1,0:T(8,128)} %convolution_add_fusion.2.refs_0_), custom_call_target="tpu_custom_call" | custom-call | tf_op jit(solution)/shard_map/pallas_call | solution.py:233
  218.1 2.4 convolution_bitcast_fusion
  220.6 1.6 fusion
  222.2 2.4 convolution_bitcast_fusion.1
  224.6 1.6 fusion.1
  226.2 0.6 fusion.69
  226.8 0.3 copy.5
  227.2 0.2 fusion.2
  227.4 1.0 copy-done.4
  228.4 0.3 copy-done.5
  228.7 1.9 pad_maximum_fusion.grad_ref
  230.7 47.8 %shard_map.48 = f32[3,64,512]{2,1,0:T(8,128)} custom-call(f32[3,512,512]{2,1,0:T(8,128)} %pad_maximum_fusion.grad_ref), custom_call_target="tpu_custom_call" | custom-call | tf_op jit(solution)/shard_map/pallas_call | solution.py:347
  279.3 2.2 fusion.56
  (15 shorter events, 0.1 us)
Async XLA Ops:
  0.0 107.3 %copy-start = (f32[256,512]{1,0:T(8,128)S(1)}, f32[256,512]{1,0:T(8,128)}, u32[]{:S(2)}) copy-start(f32[256,512]{1,0:T(8,128)} %refs_0_.1) | copy-start | bytes 1572868
  0.0 5.7 %copy-start.6 = (s32[1,3]{1,0:T(1,128)S(1)}, s32[1,3]{1,0:T(1,128)}, u32[]{:S(2)}) copy-start(s32[1,3]{1,0:T(1,128)} %param.6) | copy-start | bytes 40
  107.2 5.6 %copy-start.2 = (f32[5,256,512]{2,1,0:T(8,128)S(1)}, f32[5,256,512]{2,1,0:T(8,128)}, u32[]{:S(2)}) copy-start(f32[5,256,512]{2,1,0:T(8,128)} %get-tuple-element.8) | copy-start | bytes 7864324
  107.3 5.9 %copy-start.3 = (f32[1,3,512,512]{3,2,1,0:T(8,128)S(1)}, f32[1,3,512,512]{3,2,1,0:T(8,128)}, u32[]{:S(2)}) copy-start(f32[1,3,512,512]{3,2,1,0:T(8,128)} %param.5) | copy-start | bytes 9437188
  118.5 99.6 %copy-start.1 = (f32[256,512]{1,0:T(8,128)S(1)}, f32[256,512]{1,0:T(8,128)}, u32[]{:S(2)}) copy-start(f32[256,512]{1,0:T(8,128)} %convolution_add_fusion.2.refs_0_) | copy-start | bytes 1572868
  227.2 1.2 copy-start.4
  227.2 1.5 copy-start.5

commit v2 on v1

--- a/solution.py
+++ b/solution.py
@@ -11,6 +11,19 @@
 RING = 8
 WRAP = 2
 CHUNKS = 4
+PENALTY = 0.05
+
+
+def halves(x):
+    top = x.astype(jnp.bfloat16)
+    return top, (x - top.astype(jnp.float32)).astype(jnp.bfloat16)
+
+
+def product(left, right, left_dim, right_dim):
+    def dot(a, b):
+        return lax.dot_general(a, b, (((left_dim,), (right_dim,)), ((), ())), preferred_element_type=jnp.float32)
+
+    return dot(left[0], right[0]) + dot(left[0], right[1]) + dot(left[1], right[0])
 
 
 def var_device(index):
@@ -19,12 +32,12 @@
 
 def band_kernel(wrap, chunks, reduce_too, *refs):
     if reduce_too:
-        (data_ref, first_ref, second_ref, mask_ref, ahead_ref, carried_ref,
-         sent_ref, near_ref, far_ref, cross_ref,
+        (offset_ref, data_ref, tiles_ref, image_ref, picked_ref,
+         ahead_ref, first_ref, second_ref, top_ref, rest_ref, sent_ref, near_ref, far_ref, cross_ref,
          d_send, d_recv, d_direct, d_back,
          c_send, c_near, c_far, c_cross) = refs
     else:
-        data_ref, ahead_ref, d_send, d_recv, d_direct, d_back = refs
+        offset_ref, data_ref, picked_ref, ahead_ref, d_send, d_recv, d_direct, d_back = refs
     count = lax.axis_size("var")
     me = lax.axis_index("var")
     z = lax.rem(me, RING)
@@ -68,8 +81,18 @@
     def arrived(t, k):
         natural(t - 1, k).wait_recv()
 
+    def chosen(slot, o):
+        return jnp.where(offset_ref[0, slot] == o, 1.0, 0.0)
+
     def own(o, k):
-        return mask_ref[2 * o : 2 * o + 1] * first_ref[part(k)] + mask_ref[2 * o + 1 : 2 * o + 2] * second_ref[part(k)]
+        return chosen(1, o) * first_ref[part(k)] + chosen(2, o) * second_ref[part(k)]
+
+    def pick(k):
+        for slot in (1, 2):
+            block = chosen(slot, 1) * ahead_ref[0, part(k)]
+            for o in range(2, BAND):
+                block += chosen(slot, o) * ahead_ref[o - 1, part(k)]
+            picked_ref[slot - 1, part(k)] = block
 
     def pass_on(o, k):
         return pltpu.make_async_remote_copy(
@@ -91,9 +114,6 @@
 
     def passes(o):
         return ((z <= 6) & (z + o <= edge)) | ((z == 7) & (o <= wrap))
-
-    def has_near(o):
-        return (o < 5) & (((z >= 1) & (z + o <= edge)) | ((z == 0) & (o + 1 <= wrap)))
 
     def loop(body):
         def step(k, carry):
@@ -108,7 +128,18 @@
         def _():
             direct(k).start()
 
-        if reduce_too:
+    loop(first)
+
+    if reduce_too:
+        for slot in range(3):
+            top, rest = halves(tiles_ref[slot])
+            top_ref[slot] = top
+            rest_ref[slot] = rest
+
+        def forward(k):
+            mine = halves(data_ref[part(k)])
+            first_ref[part(k)] = product(mine, (top_ref[1], rest_ref[1]), 1, 0)
+            second_ref[part(k)] = product(mine, (top_ref[2], rest_ref[2]), 1, 0)
             sent_ref[4, part(k)] = own(5, k)
 
             @pl.when(passes(5))
@@ -120,15 +151,33 @@
                 for o in range(wrap + 1, 5):
                     sent_ref[o - 1, part(k)] = own(o, k)
                     pass_back(o, k).start()
-                if wrap < 5:
-                    pass_cross(k).start()
-
-    loop(first)
+                pass_cross(k).start()
+
+        loop(forward)
+
+        def diagonal(k):
+            image_ref[part(k)] = product(halves(data_ref[part(k)]), (top_ref[0], rest_ref[0]), 1, 0)
+
+        loop(diagonal)
 
     for tau in range(1, 6):
-        cross_t = 7 - tau
-
-        def step(k, tau=tau, cross_t=cross_t):
+        def step(k, tau=tau):
+            if reduce_too and tau <= 4:
+                o = lax.min(4, edge - z) + 1 - tau
+
+                @pl.when(o >= 1)
+                def _():
+                    @pl.when((z >= 1) | (o + 1 <= wrap))
+                    def _():
+                        pass_on(o + 1, k).wait_recv()
+                        sent_ref[o - 1, part(k)] = near_ref[o, part(k)] + own(o, k)
+
+                    @pl.when((z == 0) & (o + 1 > wrap))
+                    def _():
+                        sent_ref[o - 1, part(k)] = own(o, k)
+
+                    pass_on(o, k).start()
+
             @pl.when(z + tau <= edge)
             def _():
                 arrived(tau, k)
@@ -137,22 +186,6 @@
                 @pl.when(goes_on(tau))
                 def _():
                     natural(tau, k).start()
-
-            if reduce_too and tau <= 4:
-                o = 5 - tau
-
-                @pl.when(passes(o))
-                def _():
-                    @pl.when(has_near(o))
-                    def _():
-                        pass_on(o + 1, k).wait_recv()
-                        sent_ref[o - 1, part(k)] = near_ref[o, part(k)] + own(o, k)
-
-                    @pl.when(jnp.logical_not(has_near(o)))
-                    def _():
-                        sent_ref[o - 1, part(k)] = own(o, k)
-
-                    pass_on(o, k).start()
 
             if reduce_too and tau <= 4:
                 place = 7 - tau
@@ -166,28 +199,35 @@
                         else:
                             pass_cross(k).start()
 
-            if 2 <= tau and cross_t > wrap:
-                @pl.when(z + cross_t > edge)
-                def _():
-                    arrived(cross_t, k)
-                    if cross_t >= 2:
+            for t in {2: (5, 4), 4: (3,), 5: (2,)}.get(tau, ()):
+                if t > wrap:
+                    @pl.when(z + t > edge)
+                    def _(t=t):
+                        arrived(t, k)
+
                         @pl.when(z <= 6)
                         def _():
-                            back(cross_t, k).start()
+                            back(t, k).start()
 
         loop(step)
 
     if reduce_too:
         def final(k):
+            pick(k)
             pass_on(1, k).wait_recv()
-            carried_ref[part(k)] = near_ref[0, part(k)]
+            total = image_ref[part(k)] + near_ref[0, part(k)]
+            for slot in (1, 2):
+                total += product(halves(picked_ref[slot - 1, part(k)]), (top_ref[slot], rest_ref[slot]), 1, 1)
+            image_ref[part(k)] = total
 
             @pl.when(sends_direct)
             def _():
                 pass_cross(k).wait_recv()
-                carried_ref[part(k)] += cross_ref[part(k)]
+                image_ref[part(k)] += cross_ref[part(k)]
 
         loop(final)
+    else:
+        loop(pick)
 
     def drain(k):
         natural(0, k).wait_send()
@@ -216,28 +256,35 @@
     loop(drain)
 
 
-def band_call(data, sums, masks, wrap, chunks, reduce_too, collective_id):
+def band_call(offsets, data, tiles, wrap, chunks, collective_id):
+    reduce_too = tiles is not None
     rows, size = data.shape
     dtype = data.dtype
     sem = pltpu.SemaphoreType.DMA
-    block = jax.ShapeDtypeStruct((rows, size), dtype)
-    ahead = jax.ShapeDtypeStruct((5, rows, size), dtype)
     vm = pl.BlockSpec(memory_space=pltpu.VMEM)
+    sm = pl.BlockSpec(memory_space=pltpu.SMEM)
+    block = pltpu.VMEM((rows, size), dtype)
+    five = pltpu.VMEM((5, rows, size), dtype)
+    picked = jax.ShapeDtypeStruct((2, rows, size), dtype)
     base = [sem((5, chunks)), sem((5, chunks)), sem((chunks,)), sem((4, chunks))]
     if reduce_too:
-        scratch = [pltpu.VMEM((5, rows, size), dtype)] * 3 + [pltpu.VMEM((rows, size), dtype)] + base + [
+        halved = pltpu.VMEM(tiles.shape, jnp.bfloat16)
+        scratch = [five, block, block, halved, halved, five, five, five, block] + base + [
             sem((5, chunks)), sem((5, chunks)), sem((5, chunks)), sem((chunks,))]
-        args, outs, specs = (data, *sums, masks), (ahead, block), (vm, vm)
+        args, ins = (offsets, data, tiles), [sm, vm, vm]
+        outs, specs = (jax.ShapeDtypeStruct((rows, size), dtype), picked), (vm, vm)
     else:
-        scratch, args, outs, specs = base, (data,), ahead, vm
+        scratch = [five] + base
+        args, ins, outs, specs = (offsets, data), [sm, vm], picked, vm
     return pl.pallas_call(
         functools.partial(band_kernel, wrap, chunks, reduce_too),
-        out_shape=outs, in_specs=[vm] * len(args), out_specs=specs, scratch_shapes=scratch,
+        out_shape=outs, in_specs=ins, out_specs=specs, scratch_shapes=scratch,
         compiler_params=pltpu.CompilerParams(collective_id=collective_id, has_side_effects=True),
     )(*args)
 
 
-def sum_kernel(grad_ref, out_ref, pair_ref, sent_ref, up_ref, down_ref,
+def step_kernel(samples, offset_ref, step_ref, data_ref, image_ref, near_ref, later_ref, tiles_ref, out_ref,
+               grad_ref, pair_ref, sent_ref, up_ref, down_ref,
                p_send, p_recv, u_send, u_recv, d_send, d_recv):
     me = lax.axis_index("samp")
     core = lax.rem(me, 2)
@@ -289,7 +336,15 @@
     for j in range(places - 1):
         order += [places - 1 - j, j]
     starts = list(dict.fromkeys(order))
+    width = 2 * rows
+    data, image = halves(data_ref[...]), halves(image_ref[...])
+    rights = [(image, data)] + [(halves(later_ref[j]), halves(near_ref[j])) for j in range(2)]
     for place in starts:
+        span = slice(width * place, width * (place + 1))
+        for slot, (right_image, right_data) in enumerate(rights):
+            grad_ref[slot, span] = (
+                product([h[:, span] for h in data], right_image, 0, 0)
+                + product([h[:, span] for h in image], right_data, 0, 0))
         to_twin(place).start()
 
     for j in range(places - 1):
@@ -324,6 +379,24 @@
                 down(place).wait_recv()
                 out_ref[...] += down_ref[place]
 
+    step_size = step_ref[0]
+    start = pl.multiple_of(me * rows, rows)
+    row_ids = start + lax.broadcasted_iota(jnp.int32, out_ref.shape[1:], 0)
+    on_diag = row_ids == lax.broadcasted_iota(jnp.int32, out_ref.shape[1:], 1)
+    for slot in range(3):
+        old = tiles_ref[slot, pl.ds(start, rows)]
+        gradient = out_ref[slot] / (2.0 * samples)
+        if slot == 0:
+            gradient -= jnp.where(on_diag, 1.0 / jnp.where(on_diag, old, 1.0), 0.0)
+        stepped = old - step_size * gradient
+        bound = step_size * PENALTY
+        shrunk = jnp.where(stepped > bound, stepped - bound, jnp.where(stepped < -bound, stepped + bound, 0.0))
+        if slot == 0:
+            shrunk = jnp.where(on_diag, stepped, shrunk)
+        else:
+            shrunk = shrunk * jnp.where(offset_ref[0, slot] > 0, 1.0, 0.0)
+        out_ref[slot] = shrunk
+
     for place in range(places):
         to_twin(place).wait_send()
 
@@ -336,71 +409,29 @@
             down(place).wait_send()
 
 
-def sum_call(grad, collective_id):
-    slots, size, width = grad.shape
+def step_call(offsets, step, data, image, near, later, tiles, collective_id):
+    slots, size, width = tiles.shape
     count = lax.axis_size("samp")
     rows = size // count
     sem = pltpu.SemaphoreType.DMA
     vm = pl.BlockSpec(memory_space=pltpu.VMEM)
+    sm = pl.BlockSpec(memory_space=pltpu.SMEM)
     places = count // 2
-    buffer = pltpu.VMEM((places, slots, rows, width), grad.dtype)
+    buffer = pltpu.VMEM((places, slots, rows, width), data.dtype)
     return pl.pallas_call(
-        sum_kernel,
-        out_shape=jax.ShapeDtypeStruct((slots, rows, width), grad.dtype),
-        in_specs=[vm], out_specs=vm,
-        scratch_shapes=[buffer] * 4 + [sem((places,))] * 6,
+        functools.partial(step_kernel, data.shape[0] * count),
+        out_shape=jax.ShapeDtypeStruct((slots, rows, width), data.dtype),
+        in_specs=[sm, sm] + [vm] * 5, out_specs=vm,
+        scratch_shapes=[pltpu.VMEM((slots, size, width), data.dtype)] + [buffer] * 4 + [sem((places,))] * 6,
         compiler_params=pltpu.CompilerParams(collective_id=collective_id, has_side_effects=True),
-    )(grad)
-
-
-high = lax.Precision.HIGH
-penalty_weight = 0.05
-
-
-def product(left, right, left_dim, right_dim):
-    return lax.dot_general(left, right, (((left_dim,), (right_dim,)), ((), ())),
-                           precision=high, preferred_element_type=jnp.float32)
-
-
-def picked(offset, own, ahead):
-    block = own
-    for o in range(1, BAND):
-        block = jnp.where(offset == o, ahead[o - 1], block)
-    return block
+    )(offsets, step, data, image, near, later, tiles)
 
 
 def shards(data, tiles, offsets, step):
     tiles = tiles[0]
-    offset = offsets[0]
-    slots, size = tiles.shape[0], tiles.shape[1]
-    samp_count = lax.axis_size("samp")
-    samples = data.shape[0] * samp_count
-    step_size = step[0]
-    forward = [product(data, tiles[j], 1, 0) for j in range(slots)]
-    places = jnp.arange(16) // 2
-    slot_of_row = 1 + jnp.arange(16) % 2
-    live = ((offset[slot_of_row] == places) & (places > 0)).astype(jnp.float32)
-    masks = jnp.broadcast_to(live[:, None], (16, size))
-    ahead, carried = band_call(data, forward[1:], masks, WRAP, CHUNKS, True, 1)
-    partners = [data] + [picked(offset[j], data, ahead) for j in range(1, slots)]
-    image = forward[0] + carried
-    for j in range(1, slots):
-        image = image + product(partners[j], tiles[j], 1, 1)
-    image_ahead = band_call(image, None, None, WRAP, CHUNKS, False, 2)
-    image_partners = [image] + [picked(offset[j], image, image_ahead) for j in range(1, slots)]
-    grad = jnp.stack([product(data, image_partners[j], 0, 0) + product(image, partners[j], 0, 0) for j in range(slots)])
-    summed = sum_call(grad, 3)
-    rows = size // samp_count
-    row_start = lax.axis_index("samp") * rows
-    old = lax.dynamic_slice_in_dim(tiles, row_start, rows, 1)
-    slot_ids = jnp.arange(slots)
-    on_diag = (row_start + jnp.arange(rows))[:, None] == jnp.arange(size)[None, :]
-    diag = on_diag[None] & (slot_ids == 0)[:, None, None]
-    gradient = summed / (2.0 * samples) - jnp.where(diag, 1.0 / jnp.where(diag, old, 1.0), 0.0)
-    stepped = old - step_size * gradient
-    shrunk = jnp.sign(stepped) * jnp.maximum(jnp.abs(stepped) - step_size * penalty_weight, 0.0)
-    active = (slot_ids == 0) | (offset > 0)
-    return jnp.where(active[:, None, None], jnp.where(diag, stepped, shrunk), 0.0)[None]
+    image, near = band_call(offsets, data, tiles, WRAP, CHUNKS, 1)
+    later = band_call(offsets, image, None, WRAP, CHUNKS, 2)
+    return step_call(offsets, step, data, image, near, later, tiles, 3)[None]
 
 
 def solution(mesh):

time: 282 us -> 255 us (0.904)
  the two profiles are of different devices: /device:TPU:305 before, /device:TPU:306 now
where the time goes in v2:
time: 255 us
  Pallas kernels  252 us (99%)
    pallas_call x2, Pallas kernels, band_call(): pl.pallas_call(functools.partial(band_kernel, wrap, chunks, reduce_too),...  183 us
    pallas_call x1, Pallas kernels, step_call(): pl.pallas_call(functools.partial(step_kernel, data.shape[0] * count), out...  68.9 us

profile of v2, /device:TPU:306, one launch (start us, length us, event | category | flops | bytes accessed | tf_op | source)
XLA Modules:
  0.0 254.8 jit_solution(11528693472984203535)
XLA Ops:
  0.7 119.1 %shard_map.46 = (f32[256,512]{1,0:T(8,128)}, f32[2,256,512]{2,1,0:T(8,128)}) custom-call(s32[1,3]{1,0:T(1,128)} %offset_ref.1, f32[256,512]{1,0:T(8,128)} %data_ref.1, f32[3,512,512]{2,1,0:T(8,128)} %bitcast.2), custom_call_target="tpu_custom_call" | custom-call | tf_op jit(solution)/shard_map/pallas_call | solution.py:279
  119.7 64.3 %shard_map.47.later_ref = f32[2,256,512]{2,1,0:T(8,128)} custom-call(s32[1,3]{1,0:T(1,128)} %offset_ref.1, f32[256,512]{1,0:T(8,128)} %get-tuple-element.7.refs_1_.image_ref), custom_call_target="tpu_custom_call" | custom-call | tf_op jit(solution)/shard_map/pallas_call | solution.py:279
  184.1 68.9 %shard_map.48 = f32[3,64,512]{2,1,0:T(8,128)} custom-call(s32[1,3]{1,0:T(1,128)} %offset_ref.1, f32[1]{0:T(128)S(6)} %copy.6.step_ref, f32[256,512]{1,0:T(8,128)} %data_ref.1, f32[256,512]{1,0:T(8,128)} %get-tuple-element.7.refs_1_.image_ref, f32[2,256,512]{2,1,0:T(8,128)} %get-tuple-element.8.near_ref, f32[2,256,512]{2,1,0:T(8,128)} %shard_map.47.later_ref, ...), custom_call_target="tpu_custom_call" | custom-call | tf_op jit(solution)/shard_map/pallas_call | solution.py:421
  253.0 1.8 copy.7

commit v3 on v2

--- a/solution.py
+++ b/solution.py
@@ -9,6 +9,7 @@
 BAND = 6
 MESH = pl.DeviceIdType.MESH
 RING = 8
+WRAP_SUMS = 3
 WRAP = 2
 CHUNKS = 4
 PENALTY = 0.05
@@ -33,9 +34,9 @@
 def band_kernel(wrap, chunks, reduce_too, *refs):
     if reduce_too:
         (offset_ref, data_ref, tiles_ref, image_ref, picked_ref,
-         ahead_ref, first_ref, second_ref, top_ref, rest_ref, sent_ref, near_ref, far_ref, cross_ref,
+         ahead_ref, first_ref, second_ref, top_ref, rest_ref, sent_ref, near_ref, far_ref, cross_ref, relay_ref,
          d_send, d_recv, d_direct, d_back,
-         c_send, c_near, c_far, c_cross) = refs
+         c_send, c_near, c_far, c_cross, d_hold, d_relay) = refs
     else:
         offset_ref, data_ref, picked_ref, ahead_ref, d_send, d_recv, d_direct, d_back = refs
     count = lax.axis_size("var")
@@ -43,13 +44,15 @@
     z = lax.rem(me, RING)
     before, after = lax.rem(me + count - 1, count), lax.rem(me + 1, count)
     left5, right5 = lax.rem(me + count - 5, count), lax.rem(me + 5, count)
+    left6, right6 = lax.rem(me + count - 6, count), lax.rem(me + 6, count)
     rows = data_ref.shape[0] // chunks
     edge = 7 + wrap
 
     barrier = pltpu.get_barrier_semaphore()
-    for other in (before, after, left5, right5):
+    others = (before, after, left5, right5) + ((left6, right6) if reduce_too else ())
+    for other in others:
         pl.semaphore_signal(barrier, inc=1, device_id=var_device(other), device_id_type=MESH)
-    pl.semaphore_wait(barrier, 4)
+    pl.semaphore_wait(barrier, len(others))
 
     def part(k):
         return pl.ds(pl.multiple_of(k * rows, rows), rows)
@@ -66,6 +69,18 @@
             src_ref=data_ref.at[part(k)], dst_ref=ahead_ref.at[4, part(k)],
             send_sem=d_direct.at[k], recv_sem=d_recv.at[4, k],
             device_id=var_device(left5), device_id_type=MESH)
+
+    def direct_far(k):
+        return pltpu.make_async_remote_copy(
+            src_ref=data_ref.at[part(k)], dst_ref=relay_ref.at[part(k)],
+            send_sem=d_direct.at[k], recv_sem=d_hold.at[k],
+            device_id=var_device(left6), device_id_type=MESH)
+
+    def relay(k):
+        return pltpu.make_async_remote_copy(
+            src_ref=relay_ref.at[part(k)], dst_ref=ahead_ref.at[4, part(k)],
+            send_sem=d_relay.at[k], recv_sem=d_recv.at[4, k],
+            device_id=var_device(after), device_id_type=MESH)
 
     def back(t, k):
         return pltpu.make_async_remote_copy(
@@ -124,9 +139,18 @@
     def first(k):
         natural(0, k).start()
 
-        @pl.when(sends_direct)
-        def _():
-            direct(k).start()
+        if reduce_too:
+            @pl.when((z >= wrap) & (z <= 3))
+            def _():
+                direct(k).start()
+
+            @pl.when(z == 4)
+            def _():
+                direct_far(k).start()
+        else:
+            @pl.when(sends_direct)
+            def _():
+                direct(k).start()
 
     loop(first)
 
@@ -136,10 +160,11 @@
             top_ref[slot] = top
             rest_ref[slot] = rest
 
+        mine = halves(data_ref[...])
+        first_ref[...] = product(mine, (top_ref[1], rest_ref[1]), 1, 0)
+        second_ref[...] = product(mine, (top_ref[2], rest_ref[2]), 1, 0)
+
         def forward(k):
-            mine = halves(data_ref[part(k)])
-            first_ref[part(k)] = product(mine, (top_ref[1], rest_ref[1]), 1, 0)
-            second_ref[part(k)] = product(mine, (top_ref[2], rest_ref[2]), 1, 0)
             sent_ref[4, part(k)] = own(5, k)
 
             @pl.when(passes(5))
@@ -155,70 +180,108 @@
 
         loop(forward)
 
-        def diagonal(k):
-            image_ref[part(k)] = product(halves(data_ref[part(k)]), (top_ref[0], rest_ref[0]), 1, 0)
-
-        loop(diagonal)
-
-    for tau in range(1, 6):
-        def step(k, tau=tau):
-            if reduce_too and tau <= 4:
-                o = lax.min(4, edge - z) + 1 - tau
-
-                @pl.when(o >= 1)
+        image_ref[...] = product(mine, (top_ref[0], rest_ref[0]), 1, 0)
+
+    def move(t, k):
+        arrived(t, k)
+        natural(t, k).start()
+
+    def near_sum(o, k):
+        pass_on(o + 1, k).wait_recv()
+        sent_ref[o - 1, part(k)] = near_ref[o, part(k)] + own(o, k)
+        pass_on(o, k).start()
+
+    def far_sum(k):
+        pass_back(4, k).wait_recv()
+        sent_ref[4, part(k)] = far_ref[4, part(k)] + own(5, k)
+        pass_cross(k).start()
+
+    def sideways(k):
+        arrived(5, k)
+        back(5, k).start()
+        direct_far(k).wait_recv()
+        relay(k).start()
+
+    def plain_step(tau, k):
+        if reduce_too and tau <= 4:
+            o = 5 - tau
+            if o + 1 <= wrap:
+                near_sum(o, k)
+            else:
+                @pl.when(z >= 1)
                 def _():
-                    @pl.when((z >= 1) | (o + 1 <= wrap))
+                    near_sum(o, k)
+
+                @pl.when(z == 0)
+                def _():
+                    sent_ref[o - 1, part(k)] = own(o, k)
+                    pass_on(o, k).start()
+
+        @pl.when(z + tau <= edge)
+        def _():
+            arrived(tau, k)
+
+        if tau <= 4:
+            @pl.when(goes_on(tau))
+            def _():
+                natural(tau, k).start()
+
+        if not reduce_too:
+            for t in {2: (5, 4), 4: (3,)}.get(tau, ()):
+                @pl.when(z + t > edge)
+                def _(t=t):
+                    arrived(t, k)
+
+                    @pl.when(z <= 6)
                     def _():
-                        pass_on(o + 1, k).wait_recv()
-                        sent_ref[o - 1, part(k)] = near_ref[o, part(k)] + own(o, k)
-
-                    @pl.when((z == 0) & (o + 1 > wrap))
-                    def _():
-                        sent_ref[o - 1, part(k)] = own(o, k)
-
-                    pass_on(o, k).start()
-
-            @pl.when(z + tau <= edge)
-            def _():
-                arrived(tau, k)
-
-            if tau <= 4:
-                @pl.when(goes_on(tau))
-                def _():
-                    natural(tau, k).start()
-
-            if reduce_too and tau <= 4:
-                place = 7 - tau
-                for o in range(wrap + 1 + tau, 6):
-                    @pl.when(z == place)
-                    def _(o=o):
-                        pass_back(o - 1, k).wait_recv()
-                        sent_ref[o - 1, part(k)] = far_ref[o - 1, part(k)] + own(o, k)
-                        if o < 5:
-                            pass_back(o, k).start()
-                        else:
-                            pass_cross(k).start()
-
-            for t in {2: (5, 4), 4: (3,), 5: (2,)}.get(tau, ()):
-                if t > wrap:
-                    @pl.when(z + t > edge)
-                    def _(t=t):
-                        arrived(t, k)
-
-                        @pl.when(z <= 6)
-                        def _():
-                            back(t, k).start()
-
-        loop(step)
+                        back(t, k).start()
 
     if reduce_too:
+        @pl.when(z <= 5)
+        def _():
+            for tau in range(1, 6):
+                loop(functools.partial(plain_step, tau))
+
+        @pl.when(z == 6)
+        def _():
+            def opening(k):
+                near_sum(4, k)
+                move(1, k)
+
+            loop(opening)
+            loop(functools.partial(near_sum, 3))
+            loop(far_sum)
+            loop(functools.partial(near_sum, 2))
+            loop(functools.partial(move, 2))
+            loop(functools.partial(near_sum, 1))
+            loop(sideways)
+            loop(functools.partial(move, 3))
+            loop(functools.partial(move, 4))
+
+        @pl.when(z == 7)
+        def _():
+            loop(functools.partial(near_sum, 3))
+            loop(functools.partial(move, 1))
+            loop(functools.partial(near_sum, 2))
+            loop(functools.partial(near_sum, 1))
+            loop(functools.partial(move, 2))
+            loop(functools.partial(move, 3))
+            loop(functools.partial(arrived, 5))
+            loop(functools.partial(arrived, 4))
+    else:
+        for tau in range(1, 6):
+            loop(functools.partial(plain_step, tau))
+
+    if reduce_too:
+        loop(pick)
+        total = image_ref[...]
+        for slot in (1, 2):
+            total += product(halves(picked_ref[slot - 1]), (top_ref[slot], rest_ref[slot]), 1, 1)
+        image_ref[...] = total
+
         def final(k):
-            pick(k)
             pass_on(1, k).wait_recv()
-            total = image_ref[part(k)] + near_ref[0, part(k)]
-            for slot in (1, 2):
-                total += product(halves(picked_ref[slot - 1, part(k)]), (top_ref[slot], rest_ref[slot]), 1, 1)
-            image_ref[part(k)] = total
+            image_ref[part(k)] += near_ref[0, part(k)]
 
             @pl.when(sends_direct)
             def _():
@@ -231,6 +294,11 @@
 
     def drain(k):
         natural(0, k).wait_send()
+
+        if reduce_too:
+            @pl.when(z == 6)
+            def _():
+                relay(k).wait_send()
 
         @pl.when(sends_direct)
         def _():
@@ -269,8 +337,8 @@
     base = [sem((5, chunks)), sem((5, chunks)), sem((chunks,)), sem((4, chunks))]
     if reduce_too:
         halved = pltpu.VMEM(tiles.shape, jnp.bfloat16)
-        scratch = [five, block, block, halved, halved, five, five, five, block] + base + [
-            sem((5, chunks)), sem((5, chunks)), sem((5, chunks)), sem((chunks,))]
+        scratch = [five, block, block, halved, halved, five, five, five, block, block] + base + [
+            sem((5, chunks)), sem((5, chunks)), sem((5, chunks)), sem((chunks,)), sem((chunks,)), sem((chunks,))]
         args, ins = (offsets, data, tiles), [sm, vm, vm]
         outs, specs = (jax.ShapeDtypeStruct((rows, size), dtype), picked), (vm, vm)
     else:
@@ -429,7 +497,7 @@
 
 def shards(data, tiles, offsets, step):
     tiles = tiles[0]
-    image, near = band_call(offsets, data, tiles, WRAP, CHUNKS, 1)
+    image, near = band_call(offsets, data, tiles, WRAP_SUMS, CHUNKS, 1)
     later = band_call(offsets, image, None, WRAP, CHUNKS, 2)
     return step_call(offsets, step, data, image, near, later, tiles, 3)[None]
 

time: 255 us -> 246 us (0.965)
  the two profiles are of different devices: /device:TPU:306 before, /device:TPU:308 now
where the time goes in v3:
time: 246 us
  Pallas kernels  243 us (99%)
    pallas_call x2, Pallas kernels, band_call(): pl.pallas_call(functools.partial(band_kernel, wrap, chunks, reduce_too),...  189 us
    pallas_call x1, Pallas kernels, step_call(): pl.pallas_call(functools.partial(step_kernel, data.shape[0] * count), out...  54.7 us

profile of v3, /device:TPU:308, one launch (start us, length us, event | category | flops | bytes accessed | tf_op | source)
XLA Modules:
  0.0 245.7 jit_solution(4002517298706282484)
XLA Ops:
  0.7 110.1 %shard_map.46 = (f32[256,512]{1,0:T(8,128)}, f32[2,256,512]{2,1,0:T(8,128)}) custom-call(s32[1,3]{1,0:T(1,128)} %offset_ref.1, f32[256,512]{1,0:T(8,128)} %data_ref.1, f32[3,512,512]{2,1,0:T(8,128)} %bitcast.2), custom_call_target="tpu_custom_call" | custom-call | tf_op jit(solution)/shard_map/pallas_call | solution.py:347
  110.8 78.4 %shard_map.47.later_ref = f32[2,256,512]{2,1,0:T(8,128)} custom-call(s32[1,3]{1,0:T(1,128)} %offset_ref.1, f32[256,512]{1,0:T(8,128)} %get-tuple-element.7.refs_1_.image_ref), custom_call_target="tpu_custom_call" | custom-call | tf_op jit(solution)/shard_map/pallas_call | solution.py:347
  189.2 54.7 %shard_map.48 = f32[3,64,512]{2,1,0:T(8,128)} custom-call(s32[1,3]{1,0:T(1,128)} %offset_ref.1, f32[1]{0:T(128)S(6)} %copy.6.step_ref, f32[256,512]{1,0:T(8,128)} %data_ref.1, f32[256,512]{1,0:T(8,128)} %get-tuple-element.7.refs_1_.image_ref, f32[2,256,512]{2,1,0:T(8,128)} %get-tuple-element.8.near_ref, f32[2,256,512]{2,1,0:T(8,128)} %shard_map.47.later_ref, ...), custom_call_target="tpu_custom_call" | custom-call | tf_op jit(solution)/shard_map/pallas_call | solution.py:489
  243.9 1.8 copy.7

commit v4 on v3

--- a/solution.py
+++ b/solution.py
@@ -31,14 +31,173 @@
     return {"var": index}
 
 
+class SampleSum:
+    def __init__(self, rows, grad_ref, pair_ref, sent_ref, up_ref, down_ref,
+                 p_send, p_recv, u_send, u_recv, d_send, d_recv):
+        self.me = lax.axis_index("samp")
+        self.core = lax.rem(self.me, 2)
+        self.y = self.me // 2
+        self.places = lax.axis_size("samp") // 2
+        self.twin = self.me + 1 - 2 * self.core
+        self.rows = rows
+        self.grad_ref, self.pair_ref, self.sent_ref = grad_ref, pair_ref, sent_ref
+        self.up_ref, self.down_ref = up_ref, down_ref
+        self.sems = (p_send, p_recv, u_send, u_recv, d_send, d_recv)
+        order = []
+        for j in range(self.places - 1):
+            order += [self.places - 1 - j, j]
+        self.starts = list(dict.fromkeys(order))
+
+    def greet(self, barrier):
+        def signal(other):
+            pl.semaphore_signal(barrier, inc=1, device_id={"samp": other}, device_id_type=MESH)
+
+        signal(self.twin)
+
+        @pl.when(self.y < self.places - 1)
+        def _():
+            signal(self.me + 2)
+
+        @pl.when(self.y > 0)
+        def _():
+            signal(self.me - 2)
+
+        return 1 + lax.min(self.y, 1) + lax.min(self.places - 1 - self.y, 1)
+
+    def band(self, place, which):
+        return pl.ds(pl.multiple_of((2 * place + which) * self.rows, self.rows), self.rows)
+
+    def to_twin(self, place):
+        return pltpu.make_async_remote_copy(
+            src_ref=self.grad_ref.at[:, self.band(place, 1 - self.core)], dst_ref=self.pair_ref.at[place],
+            send_sem=self.sems[0].at[place], recv_sem=self.sems[1].at[place],
+            device_id={"samp": self.twin}, device_id_type=MESH)
+
+    def up(self, place):
+        return pltpu.make_async_remote_copy(
+            src_ref=self.sent_ref.at[place], dst_ref=self.up_ref.at[place],
+            send_sem=self.sems[2].at[place], recv_sem=self.sems[3].at[place],
+            device_id={"samp": self.me + 2}, device_id_type=MESH)
+
+    def down(self, place):
+        return pltpu.make_async_remote_copy(
+            src_ref=self.sent_ref.at[place], dst_ref=self.down_ref.at[place],
+            send_sem=self.sems[4].at[place], recv_sem=self.sems[5].at[place],
+            device_id={"samp": self.me - 2}, device_id_type=MESH)
+
+    def stage(self, j):
+        y, places = self.y, self.places
+        for rising in (True, False):
+            place = places - 1 - j if rising else j
+
+            @pl.when(y < place if rising else y > place)
+            def _(place=place, rising=rising):
+                self.to_twin(place).wait_recv()
+                self.sent_ref[place] = self.grad_ref[:, self.band(place, self.core)] + self.pair_ref[place]
+
+                @pl.when(y > 0 if rising else y < places - 1)
+                def _():
+                    if rising:
+                        self.up(place).wait_recv()
+                        self.sent_ref[place] += self.up_ref[place]
+                    else:
+                        self.down(place).wait_recv()
+                        self.sent_ref[place] += self.down_ref[place]
+
+                (self.up if rising else self.down)(place).start()
+
+    def finish(self, out_ref):
+        for place in range(self.places):
+            @pl.when(self.y == place)
+            def _(place=place):
+                self.to_twin(place).wait_recv()
+                total = self.grad_ref[:, self.band(place, self.core)] + self.pair_ref[place]
+                if place > 0:
+                    self.up(place).wait_recv()
+                    total += self.up_ref[place]
+                if place < self.places - 1:
+                    self.down(place).wait_recv()
+                    total += self.down_ref[place]
+                out_ref[...] = total
+
+    def drain(self):
+        for place in range(self.places):
+            self.to_twin(place).wait_send()
+
+            @pl.when(self.y < place)
+            def _(place=place):
+                self.up(place).wait_send()
+
+            @pl.when(self.y > place)
+            def _(place=place):
+                self.down(place).wait_send()
+
+
+def sum_scratch(slots, size, rows, places, dtype):
+    buffer = pltpu.VMEM((places, slots, rows, size), dtype)
+    return [pltpu.VMEM((slots, size, size), dtype)] + [buffer] * 4 + [pltpu.SemaphoreType.DMA((places,))] * 6
+
+
+def step_kernel(samples, offset_ref, step_ref, data_ref, later_ref, rest_ref, done_ref, tiles_ref, out_ref,
+                old_ref, total_ref, old_sem, *refs):
+    rows = out_ref.shape[1]
+    half = len(refs) // 2
+    sums = [SampleSum(rows, *refs[:half]), SampleSum(rows, *refs[half:])]
+    start = pl.multiple_of(sums[0].me * rows, rows)
+    old_copy = pltpu.make_async_copy(tiles_ref.at[:, pl.ds(start, rows)], old_ref, old_sem)
+    old_copy.start()
+    barrier = pltpu.get_barrier_semaphore()
+    peers = sums[0].greet(barrier)
+    pl.semaphore_wait(barrier, peers)
+
+    width = 2 * rows
+    data = halves(data_ref[...])
+    for slot, one in enumerate(sums):
+        right = halves(later_ref[slot])
+        for place in one.starts:
+            span = slice(width * place, width * (place + 1))
+            one.grad_ref[0, span] = product([h[:, span] for h in data], right, 0, 0) + rest_ref[slot, span]
+            one.to_twin(place).start()
+
+    for j in range(sums[0].places - 1):
+        for one in sums:
+            one.stage(j)
+    for slot, one in enumerate(sums):
+        one.finish(total_ref.at[pl.ds(slot, 1)])
+    old_copy.wait()
+
+    step_size = step_ref[0]
+    bound = step_size * PENALTY
+    row_ids = start + lax.broadcasted_iota(jnp.int32, out_ref.shape[1:], 0)
+    on_diag = row_ids == lax.broadcasted_iota(jnp.int32, out_ref.shape[1:], 1)
+    for slot in range(3):
+        old = old_ref[slot]
+        gradient = (done_ref[0] if slot == 0 else total_ref[slot - 1]) / (2.0 * samples)
+        if slot == 0:
+            gradient -= jnp.where(on_diag, 1.0 / jnp.where(on_diag, old, 1.0), 0.0)
+        stepped = old - step_size * gradient
+        shrunk = jnp.where(stepped > bound, stepped - bound, jnp.where(stepped < -bound, stepped + bound, 0.0))
+        if slot == 0:
+            shrunk = jnp.where(on_diag, stepped, shrunk)
+        else:
+            shrunk = shrunk * jnp.where(offset_ref[0, slot] > 0, 1.0, 0.0)
+        out_ref[slot] = shrunk
+
+    for one in sums:
+        one.drain()
+
+
 def band_kernel(wrap, chunks, reduce_too, *refs):
     if reduce_too:
-        (offset_ref, data_ref, tiles_ref, image_ref, picked_ref,
+        (offset_ref, data_ref, tiles_hbm, image_ref, picked_ref,
+         tiles_ref, tiles_sem,
          ahead_ref, first_ref, second_ref, top_ref, rest_ref, sent_ref, near_ref, far_ref, cross_ref, relay_ref,
          d_send, d_recv, d_direct, d_back,
          c_send, c_near, c_far, c_cross, d_hold, d_relay) = refs
     else:
-        offset_ref, data_ref, picked_ref, ahead_ref, d_send, d_recv, d_direct, d_back = refs
+        (offset_ref, data_ref, first_data_ref, first_picked_ref, picked_ref, rest_out_ref, done_ref,
+         ahead_ref, d_send, d_recv, d_direct, d_back, *sum_refs) = refs
+        sums = SampleSum(done_ref.shape[1], *sum_refs)
     count = lax.axis_size("var")
     me = lax.axis_index("var")
     z = lax.rem(me, RING)
@@ -48,11 +207,17 @@
     rows = data_ref.shape[0] // chunks
     edge = 7 + wrap
 
+    if reduce_too:
+        tiles_copy = pltpu.make_async_copy(tiles_hbm, tiles_ref, tiles_sem)
+        tiles_copy.start()
     barrier = pltpu.get_barrier_semaphore()
     others = (before, after, left5, right5) + ((left6, right6) if reduce_too else ())
     for other in others:
         pl.semaphore_signal(barrier, inc=1, device_id=var_device(other), device_id_type=MESH)
-    pl.semaphore_wait(barrier, len(others))
+    greeted = len(others)
+    if not reduce_too:
+        greeted = greeted + sums.greet(barrier)
+    pl.semaphore_wait(barrier, greeted)
 
     def part(k):
         return pl.ds(pl.multiple_of(k * rows, rows), rows)
@@ -155,6 +320,7 @@
     loop(first)
 
     if reduce_too:
+        tiles_copy.wait()
         for slot in range(3):
             top, rest = halves(tiles_ref[slot])
             top_ref[slot] = top
@@ -269,8 +435,17 @@
             loop(functools.partial(arrived, 5))
             loop(functools.partial(arrived, 4))
     else:
+        image, data = halves(data_ref[...]), halves(first_data_ref[...])
+        sums.grad_ref[0] = product(data, image, 0, 0) + product(image, data, 0, 0)
+        for place in sums.starts:
+            sums.to_twin(place).start()
+        for slot in range(2):
+            rest_out_ref[slot] = product(image, halves(first_picked_ref[slot]), 0, 0)
         for tau in range(1, 6):
             loop(functools.partial(plain_step, tau))
+            for j in range(3):
+                if tau == (3, 4, 5)[j]:
+                    sums.stage(j)
 
     if reduce_too:
         loop(pick)
@@ -291,6 +466,8 @@
         loop(final)
     else:
         loop(pick)
+        sums.finish(done_ref)
+        sums.drain()
 
     def drain(k):
         natural(0, k).wait_send()
@@ -324,7 +501,7 @@
     loop(drain)
 
 
-def band_call(offsets, data, tiles, wrap, chunks, collective_id):
+def band_call(offsets, data, tiles, earlier, wrap, chunks, collective_id):
     reduce_too = tiles is not None
     rows, size = data.shape
     dtype = data.dtype
@@ -337,13 +514,16 @@
     base = [sem((5, chunks)), sem((5, chunks)), sem((chunks,)), sem((4, chunks))]
     if reduce_too:
         halved = pltpu.VMEM(tiles.shape, jnp.bfloat16)
-        scratch = [five, block, block, halved, halved, five, five, five, block, block] + base + [
+        scratch = [pltpu.VMEM(tiles.shape, dtype), sem, five, block, block, halved, halved, five, five, five, block, block] + base + [
             sem((5, chunks)), sem((5, chunks)), sem((5, chunks)), sem((chunks,)), sem((chunks,)), sem((chunks,))]
-        args, ins = (offsets, data, tiles), [sm, vm, vm]
+        args, ins = (offsets, data, tiles), [sm, vm, pl.BlockSpec(memory_space=pl.ANY)]
         outs, specs = (jax.ShapeDtypeStruct((rows, size), dtype), picked), (vm, vm)
     else:
-        scratch = [five] + base
-        args, ins, outs, specs = (offsets, data), [sm, vm], picked, vm
+        count = lax.axis_size("samp")
+        scratch = [five] + base + sum_scratch(1, size, size // count, count // 2, dtype)
+        args, ins = (offsets, data, *earlier), [sm, vm, vm, vm]
+        outs = (picked, jax.ShapeDtypeStruct((2, size, size), dtype), jax.ShapeDtypeStruct((1, size // count, size), dtype))
+        specs = (vm, vm, vm)
     return pl.pallas_call(
         functools.partial(band_kernel, wrap, chunks, reduce_too),
         out_shape=outs, in_specs=ins, out_specs=specs, scratch_shapes=scratch,
@@ -351,155 +531,28 @@
     )(*args)
 
 
-def step_kernel(samples, offset_ref, step_ref, data_ref, image_ref, near_ref, later_ref, tiles_ref, out_ref,
-               grad_ref, pair_ref, sent_ref, up_ref, down_ref,
-               p_send, p_recv, u_send, u_recv, d_send, d_recv):
-    me = lax.axis_index("samp")
-    core = lax.rem(me, 2)
-    y = me // 2
-    places = lax.axis_size("samp") // 2
-    rows = out_ref.shape[1]
-    twin = me + 1 - 2 * core
-
-    barrier = pltpu.get_barrier_semaphore()
-
-    def greet(other):
-        pl.semaphore_signal(barrier, inc=1, device_id={"samp": other}, device_id_type=MESH)
-
-    greet(twin)
-
-    @pl.when(y < places - 1)
-    def _():
-        greet(me + 2)
-
-    @pl.when(y > 0)
-    def _():
-        greet(me - 2)
-
-    peers = 1 + lax.min(y, 1) + lax.min(places - 1 - y, 1)
-    pl.semaphore_wait(barrier, peers)
-
-    def band(place, which):
-        return pl.ds(pl.multiple_of((2 * place + which) * rows, rows), rows)
-
-    def to_twin(place):
-        return pltpu.make_async_remote_copy(
-            src_ref=grad_ref.at[:, band(place, 1 - core)], dst_ref=pair_ref.at[place],
-            send_sem=p_send.at[place], recv_sem=p_recv.at[place],
-            device_id={"samp": twin}, device_id_type=MESH)
-
-    def up(place):
-        return pltpu.make_async_remote_copy(
-            src_ref=sent_ref.at[place], dst_ref=up_ref.at[place],
-            send_sem=u_send.at[place], recv_sem=u_recv.at[place],
-            device_id={"samp": me + 2}, device_id_type=MESH)
-
-    def down(place):
-        return pltpu.make_async_remote_copy(
-            src_ref=sent_ref.at[place], dst_ref=down_ref.at[place],
-            send_sem=d_send.at[place], recv_sem=d_recv.at[place],
-            device_id={"samp": me - 2}, device_id_type=MESH)
-
-    order = []
-    for j in range(places - 1):
-        order += [places - 1 - j, j]
-    starts = list(dict.fromkeys(order))
-    width = 2 * rows
-    data, image = halves(data_ref[...]), halves(image_ref[...])
-    rights = [(image, data)] + [(halves(later_ref[j]), halves(near_ref[j])) for j in range(2)]
-    for place in starts:
-        span = slice(width * place, width * (place + 1))
-        for slot, (right_image, right_data) in enumerate(rights):
-            grad_ref[slot, span] = (
-                product([h[:, span] for h in data], right_image, 0, 0)
-                + product([h[:, span] for h in image], right_data, 0, 0))
-        to_twin(place).start()
-
-    for j in range(places - 1):
-        for rising in (True, False):
-            place = places - 1 - j if rising else j
-
-            @pl.when(y < place if rising else y > place)
-            def _(place=place, rising=rising):
-                to_twin(place).wait_recv()
-                sent_ref[place] = grad_ref[:, band(place, core)] + pair_ref[place]
-
-                @pl.when(y > 0 if rising else y < places - 1)
-                def _():
-                    if rising:
-                        up(place).wait_recv()
-                        sent_ref[place] += up_ref[place]
-                    else:
-                        down(place).wait_recv()
-                        sent_ref[place] += down_ref[place]
-
-                (up if rising else down)(place).start()
-
-    for place in range(places):
-        @pl.when(y == place)
-        def _(place=place):
-            to_twin(place).wait_recv()
-            out_ref[...] = grad_ref[:, band(place, core)] + pair_ref[place]
-            if place > 0:
-                up(place).wait_recv()
-                out_ref[...] += up_ref[place]
-            if place < places - 1:
-                down(place).wait_recv()
-                out_ref[...] += down_ref[place]
-
-    step_size = step_ref[0]
-    start = pl.multiple_of(me * rows, rows)
-    row_ids = start + lax.broadcasted_iota(jnp.int32, out_ref.shape[1:], 0)
-    on_diag = row_ids == lax.broadcasted_iota(jnp.int32, out_ref.shape[1:], 1)
-    for slot in range(3):
-        old = tiles_ref[slot, pl.ds(start, rows)]
-        gradient = out_ref[slot] / (2.0 * samples)
-        if slot == 0:
-            gradient -= jnp.where(on_diag, 1.0 / jnp.where(on_diag, old, 1.0), 0.0)
-        stepped = old - step_size * gradient
-        bound = step_size * PENALTY
-        shrunk = jnp.where(stepped > bound, stepped - bound, jnp.where(stepped < -bound, stepped + bound, 0.0))
-        if slot == 0:
-            shrunk = jnp.where(on_diag, stepped, shrunk)
-        else:
-            shrunk = shrunk * jnp.where(offset_ref[0, slot] > 0, 1.0, 0.0)
-        out_ref[slot] = shrunk
-
-    for place in range(places):
-        to_twin(place).wait_send()
-
-        @pl.when(y < place)
-        def _(place=place):
-            up(place).wait_send()
-
-        @pl.when(y > place)
-        def _(place=place):
-            down(place).wait_send()
-
-
-def step_call(offsets, step, data, image, near, later, tiles, collective_id):
+def step_call(offsets, step, data, later, rest, done, tiles, collective_id):
     slots, size, width = tiles.shape
     count = lax.axis_size("samp")
     rows = size // count
-    sem = pltpu.SemaphoreType.DMA
     vm = pl.BlockSpec(memory_space=pltpu.VMEM)
     sm = pl.BlockSpec(memory_space=pltpu.SMEM)
-    places = count // 2
-    buffer = pltpu.VMEM((places, slots, rows, width), data.dtype)
+    dtype = data.dtype
     return pl.pallas_call(
         functools.partial(step_kernel, data.shape[0] * count),
-        out_shape=jax.ShapeDtypeStruct((slots, rows, width), data.dtype),
-        in_specs=[sm, sm] + [vm] * 5, out_specs=vm,
-        scratch_shapes=[pltpu.VMEM((slots, size, width), data.dtype)] + [buffer] * 4 + [sem((places,))] * 6,
+        out_shape=jax.ShapeDtypeStruct((slots, rows, width), dtype),
+        in_specs=[sm, sm] + [vm] * 4 + [pl.BlockSpec(memory_space=pl.ANY)], out_specs=vm,
+        scratch_shapes=[pltpu.VMEM((slots, rows, width), dtype), pltpu.VMEM((2, rows, width), dtype),
+                        pltpu.SemaphoreType.DMA] + sum_scratch(1, size, rows, count // 2, dtype) * 2,
         compiler_params=pltpu.CompilerParams(collective_id=collective_id, has_side_effects=True),
-    )(offsets, step, data, image, near, later, tiles)
+    )(offsets, step, data, later, rest, done, tiles)
 
 
 def shards(data, tiles, offsets, step):
     tiles = tiles[0]
-    image, near = band_call(offsets, data, tiles, WRAP_SUMS, CHUNKS, 1)
-    later = band_call(offsets, image, None, WRAP, CHUNKS, 2)
-    return step_call(offsets, step, data, image, near, later, tiles, 3)[None]
+    image, near = band_call(offsets, data, tiles, None, WRAP_SUMS, CHUNKS, 1)
+    later, rest, done = band_call(offsets, image, None, (data, near), WRAP, CHUNKS, 2)
+    return step_call(offsets, step, data, later, rest, done, tiles, 3)[None]
 
 
 def solution(mesh):

time: 246 us -> 242 us (0.984)
  the two profiles are of different devices: /device:TPU:308 before, /device:TPU:336 now
where the time goes in v4:
time: 242 us
  Pallas kernels  239 us (99%)
    pallas_call x2, Pallas kernels, band_call(): pl.pallas_call(functools.partial(band_kernel, wrap, chunks, reduce_too),...  203 us
    pallas_call x1, Pallas kernels, step_call(): pl.pallas_call(functools.partial(step_kernel, data.shape[0] * count), out...  36.4 us

profile of v4, /device:TPU:336, one launch (start us, length us, event | category | flops | bytes accessed | tf_op | source)
XLA Modules:
  0.0 241.7 jit_solution(3930718649873215924)
XLA Ops:
  0.0 115.5 %shard_map.46 = (f32[256,512]{1,0:T(8,128)}, f32[2,256,512]{2,1,0:T(8,128)}) custom-call(s32[1,3]{1,0:T(1,128)} %offset_ref.1, f32[256,512]{1,0:T(8,128)} %data_ref.1, f32[3,512,512]{2,1,0:T(8,128)} %bitcast.2), custom_call_target="tpu_custom_call" | custom-call | tf_op jit(solution)/shard_map/pallas_call | solution.py:527
  115.5 87.4 %shard_map.47 = (f32[2,256,512]{2,1,0:T(8,128)}, f32[2,512,512]{2,1,0:T(8,128)}, f32[1,64,512]{2,1,0:T(8,128)}) custom-call(s32[1,3]{1,0:T(1,128)} %offset_ref.1, f32[256,512]{1,0:T(8,128)} %get-tuple-element.10.refs_1_, f32[256,512]{1,0:T(8,128)} %data_ref.1, f32[2,256,512]{2,1,0:T(8,128)} %get-tuple-element.11.refs_3_), custom_call_target="tpu_custom_call" | custom-call | tf_op jit(solution)/shard_map/pallas_call | solution.py:527
  203.6 36.4 %shard_map.48 = f32[3,64,512]{2,1,0:T(8,128)} custom-call(s32[1,3]{1,0:T(1,128)} %offset_ref.1, f32[1]{0:T(128)S(6)} %copy.6.step_ref, f32[256,512]{1,0:T(8,128)} %data_ref.1, f32[2,256,512]{2,1,0:T(8,128)} %get-tuple-element.12.later_ref, f32[2,512,512]{2,1,0:T(8,128)} %get-tuple-element.13.rest_ref, f32[1,64,512]{2,1,0:T(8,128)} %get-tuple-element.14.done_ref, ...), custom_call_target="tpu_custom_call" | custom-call | tf_op jit(solution)/shard_map/pallas_call | solution.py:541
  240.0 1.8 copy.7

commit v5 on v4

--- a/solution.py
+++ b/solution.py
@@ -309,9 +309,6 @@
             def _():
                 direct(k).start()
 
-            @pl.when(z == 4)
-            def _():
-                direct_far(k).start()
         else:
             @pl.when(sends_direct)
             def _():
@@ -406,6 +403,11 @@
         @pl.when(z <= 5)
         def _():
             for tau in range(1, 6):
+                if tau == 3:
+                    @pl.when(z == 4)
+                    def _():
+                        loop(lambda k: direct_far(k).start())
+
                 loop(functools.partial(plain_step, tau))
 
         @pl.when(z == 6)

time: 242 us -> 242 us (level)
  the two profiles are of different devices: /device:TPU:336 before, /device:TPU:308 now
where the time goes in v5:
time: 242 us; the launch traced here: 241 us
  Pallas kernels  239 us (99%)
    pallas_call x2, Pallas kernels, band_call(): pl.pallas_call(functools.partial(band_kernel, wrap, chunks, reduce_too),...  198 us
    pallas_call x1, Pallas kernels, step_call(): pl.pallas_call(functools.partial(step_kernel, data.shape[0] * count), out...  40.9 us

profile of v5, /device:TPU:308, one launch (start us, length us, event | category | flops | bytes accessed | tf_op | source)
XLA Modules:
  0.0 241.4 jit_solution(9911263309408513162)
XLA Ops:
  0.0 101.2 %shard_map.46 = (f32[256,512]{1,0:T(8,128)}, f32[2,256,512]{2,1,0:T(8,128)}) custom-call(s32[1,3]{1,0:T(1,128)} %offset_ref.1, f32[256,512]{1,0:T(8,128)} %data_ref.1, f32[3,512,512]{2,1,0:T(8,128)} %bitcast.2), custom_call_target="tpu_custom_call" | custom-call | tf_op jit(solution)/shard_map/pallas_call | solution.py:529
  101.2 96.8 %shard_map.47 = (f32[2,256,512]{2,1,0:T(8,128)}, f32[2,512,512]{2,1,0:T(8,128)}, f32[1,64,512]{2,1,0:T(8,128)}) custom-call(s32[1,3]{1,0:T(1,128)} %offset_ref.1, f32[256,512]{1,0:T(8,128)} %get-tuple-element.10.refs_1_, f32[256,512]{1,0:T(8,128)} %data_ref.1, f32[2,256,512]{2,1,0:T(8,128)} %get-tuple-element.11.refs_3_), custom_call_target="tpu_custom_call" | custom-call | tf_op jit(solution)/shard_map/pallas_call | solution.py:529
  198.7 40.9 %shard_map.48 = f32[3,64,512]{2,1,0:T(8,128)} custom-call(s32[1,3]{1,0:T(1,128)} %offset_ref.1, f32[1]{0:T(128)S(6)} %copy.6.step_ref, f32[256,512]{1,0:T(8,128)} %data_ref.1, f32[2,256,512]{2,1,0:T(8,128)} %get-tuple-element.12.later_ref, f32[2,512,512]{2,1,0:T(8,128)} %get-tuple-element.13.rest_ref, f32[1,64,512]{2,1,0:T(8,128)} %get-tuple-element.14.done_ref, ...), custom_call_target="tpu_custom_call" | custom-call | tf_op jit(solution)/shard_map/pallas_call | solution.py:543
  239.7 1.8 copy.7
